TPU v7x, 32 devices: a whole 2x2x4 slice. The times are simulated.
32 devices in a mesh: dp: 8 (over z, x), expert: 4 (over y, core).
Axes of the slice: x: 2, y: 2, z: 4, core: 2. Of those that a mesh axis runs over, the one named last changes fastest.
Arguments:
- tokens: bfloat16 [4096, 2048], P(('dp', 'expert')), may hold values from -6 to 6
- d_out: bfloat16 [4096, 2048], P(('dp', 'expert')), may hold values from -6 to 6
- routes: int32 [4096, 2], P(('dp', 'expert')), may hold values from 0 to 3, all different within a row; in each aligned block of 128 rows (0 to 127, 128 to 255, ...) at most 96 rows name the same one
- gate_fixed: int32 [4096, 2], P(('dp', 'expert')), may hold values from 1 to 65535
- w_gate: bfloat16 [4, 2048, 768], P('expert'), may hold values from -0.125 to 0.125
- w_up: bfloat16 [4, 2048, 768], P('expert'), may hold values from -0.125 to 0.125
- w_down: bfloat16 [4, 768, 2048], P('expert'), may hold values from -0.21875 to 0.21875
Outputs:
- d_tokens: bfloat16 [4096, 2048], P(('dp', 'expert'))
- d_wgate: float32 [4, 2048, 768], P('expert', 'dp')
- d_wup: float32 [4, 2048, 768], P('expert', 'dp')
- d_wdown: float32 [4, 768, 2048], P('expert', 'dp')
Inputs may be any that keep to these rules, and one draw needn't show every extreme that they name: Each token names 2 different experts; of the routes of one device's 128 tokens (aligned blocks of rows) at most 96 name any one expert, a bound that some block reaches of them.
All inputs are finite; a program needn't handle non-finite values.
Results may differ from a plain program's by a relative error of at most 0.0065.
Values may be sent and summed in bfloat16 or wider, within the bound.
A program may use at most 192 MiB of HBM per device.

v0:
```python
import jax
import jax.numpy as jnp
from jax import lax
from jax.sharding import PartitionSpec as P


def forward_part(rows_x, w_gate, w_up):
    pre_gate = jnp.einsum("erd,edi->eri", rows_x, w_gate, preferred_element_type=jnp.float32)
    pre_up = jnp.einsum("erd,edi->eri", rows_x, w_up, preferred_element_type=jnp.float32)
    return (pre_gate, pre_up)


def backward_part(pre_gate, pre_up, scaled, w_gate, w_up, w_down):
    sigmoid_gate = jax.nn.sigmoid(pre_gate)
    silu_gate = pre_gate * sigmoid_gate
    hidden = (silu_gate * pre_up).astype(jnp.bfloat16)
    d_hidden = jnp.einsum("erd,eid->eri", scaled, w_down, preferred_element_type=jnp.float32)
    d_gate = (d_hidden * pre_up * sigmoid_gate * (1.0 + pre_gate * (1.0 - sigmoid_gate))).astype(
        jnp.bfloat16
    )
    d_up = (d_hidden * silu_gate).astype(jnp.bfloat16)
    route_grad = (
        jnp.einsum("eri,edi->erd", d_gate, w_gate, preferred_element_type=jnp.float32)
        + jnp.einsum("eri,edi->erd", d_up, w_up, preferred_element_type=jnp.float32)
    ).astype(jnp.bfloat16)
    return (hidden, d_gate, d_up, route_grad)


def body(tokens, d_out, routes, gate_fixed, w_gate, w_up, w_down):
    expert_span = lax.axis_size("expert")
    replicas = lax.axis_size("dp")
    local_count = w_gate.shape[0]
    expert_total = expert_span * local_count
    token_count, top_count = routes.shape
    model_width = tokens.shape[1]
    hidden_units = w_gate.shape[2]
    capacity = 3 * token_count * top_count // (2 * expert_total)
    inverse = 1.0 / replicas
    expert_ids = routes.reshape(-1)
    one_hot = (expert_ids[:, None] == jnp.arange(expert_total, dtype=jnp.int32)[None, :]).astype(
        jnp.int32
    )
    earlier = jnp.cumsum(one_hot, axis=0) - one_hot
    slot_index = jnp.sum(earlier * one_hot, axis=1)
    target = expert_ids * capacity + slot_index
    placing = (
        target[:, None] == jnp.arange(expert_total * capacity, dtype=jnp.int32)[None, :]
    ).astype(jnp.bfloat16)
    token_placing = jnp.sum(placing.reshape(token_count, top_count, -1), axis=1)
    gate_value = gate_fixed.astype(jnp.float32) / 65536.0
    scaled_routes = (gate_value[:, :, None] * d_out[:, None, :].astype(jnp.float32)).astype(
        jnp.bfloat16
    )
    scaled_routes = scaled_routes.reshape(-1, model_width)
    send_x = jnp.einsum("ts,td->sd", token_placing, tokens, preferred_element_type=jnp.float32)
    send_x = send_x.astype(jnp.bfloat16).reshape(expert_total, capacity, model_width)
    send_scaled = jnp.einsum(
        "rs,rd->sd", placing, scaled_routes, preferred_element_type=jnp.float32
    )
    send_scaled = send_scaled.astype(jnp.bfloat16).reshape(expert_total, capacity, model_width)
    rows_x, scaled = (
        lax.all_to_all(send_x, "expert", split_axis=0, concat_axis=1, tiled=True),
        lax.all_to_all(send_scaled, "expert", split_axis=0, concat_axis=1, tiled=True),
    )
    pre_gate, pre_up = forward_part(rows_x, w_gate, w_up)
    hidden, d_gate, d_up, route_grad = backward_part(pre_gate, pre_up, scaled, w_gate, w_up, w_down)
    returned = lax.all_to_all(route_grad, "expert", split_axis=1, concat_axis=0, tiled=True)
    route_rows = jnp.einsum(
        "rs,sd->rd", placing, returned.reshape(-1, model_width), preferred_element_type=jnp.float32
    )
    d_tokens = jnp.sum(route_rows.reshape(token_count, top_count, model_width), axis=1).astype(
        jnp.bfloat16
    )
    stacked = jnp.concatenate([d_gate, d_up], axis=2)
    feature_rows = model_width // replicas
    split_rows = rows_x.reshape(local_count, rows_x.shape[1], replicas, feature_rows)
    columns = lax.all_to_all(split_rows, "dp", split_axis=2, concat_axis=1, tiled=True)
    columns = columns.reshape(local_count, -1, feature_rows)
    reduced = (
        jnp.einsum(
            "erc,erj->cej",
            columns,
            lax.all_gather(stacked, "dp", axis=1, tiled=True),
            preferred_element_type=jnp.float32,
        )
        * inverse
    )
    d_wgate = jnp.transpose(reduced[:, :, :hidden_units], (1, 0, 2))
    d_wup = jnp.transpose(reduced[:, :, hidden_units:], (1, 0, 2))
    down_reduced = lax.psum_scatter(
        jnp.einsum("erc,erd->ced", hidden, scaled, preferred_element_type=jnp.float32) * inverse,
        "dp",
        scatter_dimension=0,
        tiled=True,
    )
    d_wdown = jnp.transpose(down_reduced, (1, 0, 2))
    return (d_tokens, d_wgate, d_wup, d_wdown)


def solution(mesh):
    in_specs = (
        P(("dp", "expert"), None),
        P(("dp", "expert"), None),
        P(("dp", "expert"), None),
        P(("dp", "expert"), None),
        P("expert", None, None),
        P("expert", None, None),
        P("expert", None, None),
    )
    out_specs = (
        P(("dp", "expert"), None),
        P("expert", "dp", None),
        P("expert", "dp", None),
        P("expert", "dp", None),
    )
    return jax.shard_map(body, mesh=mesh, in_specs=in_specs, out_specs=out_specs, check_vma=False)
```

profile of v0, /device:TPU:20, one launch (start us, length us, event | category | flops | bytes accessed | tf_op | source)
XLA Modules:
  0.0 475.9 jit_solution(15510985037377215370)
XLA Ops:
  7.2 0.0 copy-start
  7.2 0.9 copy.83
  8.1 0.1 eq.71
  8.3 0.1 eq.67
  8.4 1.2 reduce-window.6
  9.6 0.1 slice.16
  9.7 0.1 copy.85
  9.9 0.1 copy.86
  10.0 0.1 add_bitcast_fusion
  10.1 0.1 reduce_sum.33
  10.2 0.1 copy.87
  10.3 0.7 multiply_add_fusion.1
  11.0 0.1 fusion.35
  11.1 2.8 convolution_convert_fusion
  13.9 4.8 %all-to-all-start.1 = ((bf16[4,96,2048]{2,1,0:T(8,128)(2,1)}), bf16[4,96,2048]{2,1,0:T(8,128)(2,1)}, u32[]{:S(2)}, u32[]{:S(2)}) async-start(bf16[4,96,2048]{2,1,0:T(8,128)(2,1)} %bitcast.99), calls=%async_computation.1 | async-start | bytes 3145728 | tf_op jit(solution)/shard_map/all_to_all | solution.py:62
  18.7 3.4 mul.95
  22.1 3.7 mul.96
  25.8 0.0 copy-done.5
  25.8 0.1 copy.88
  26.0 0.1 mul.93
  26.1 3.4 convolution_convert_fusion.1
  29.5 7.7 %all-to-all-done.1 = bf16[4,96,2048]{2,1,0:T(8,128)(2,1)} async-done(((bf16[4,96,2048]{2,1,0:T(8,128)(2,1)}), bf16[4,96,2048]{2,1,0:T(8,128)(2,1)}, u32[]{:S(2)}, u32[]{:S(2)}) %all-to-all-start.1) | async-done | bytes 1572896 | tf_op jit(solution)/shard_map/all_to_all | solution.py:62
  37.2 6.0 %all-to-all-start = ((bf16[4,96,2048]{2,1,0:T(8,128)(2,1)}), bf16[4,96,2048]{2,1,0:T(8,128)(2,1)}, u32[]{:S(2)}, u32[]{:S(2)}) async-start(bf16[4,96,2048]{2,1,0:T(8,128)(2,1)} %bitcast.100), calls=%async_computation | async-start | bytes 3145728 | tf_op jit(solution)/shard_map/all_to_all | solution.py:63
  43.2 0.0 all-reduce.3.cloned.1.call-start
  43.2 0.0 copy-done
  43.2 4.1 fusion.4
  47.3 3.8 fusion.8
  51.2 10.6 %all-to-all-done = bf16[4,96,2048]{2,1,0:T(8,128)(2,1)} async-done(((bf16[4,96,2048]{2,1,0:T(8,128)(2,1)}), bf16[4,96,2048]{2,1,0:T(8,128)(2,1)}, u32[]{:S(2)}, u32[]{:S(2)}) %all-to-all-start) | async-done | bytes 1572896 | tf_op jit(solution)/shard_map/all_to_all | solution.py:63
  61.8 6.7 %multiply_bitcast_fusion = f32[768,1,2048]{0,2,1:T(8,128)} fusion(bf16[384,2048]{1,0:T(8,128)(2,1)} %bitcast.4, f32[384,768]{1,0:T(8,128)} %fusion.8, f32[384,768]{1,0:T(8,128)} %fusion.4), kind=kOutput, calls=%fused_computation.2 | convolution fusion | flops 1211301888 | bytes 10223616 | tf_op jit(solution)/shard_map/erc,erd->ced/dot_general | solution.py:91
  68.4 15.9 %copy.91 = f32[768,1,2048]{2,1,0:T(1,128)} copy(f32[768,1,2048]{0,2,1:T(8,128)} %multiply_bitcast_fusion) | data formatting | bytes 12582912 | tf_op jit(solution)/shard_map/mul | solution.py:91
  84.4 0.0 all-reduce.3.cloned.1.call-update
  84.4 0.2 all-gather.2.cloned.1.call-start
  84.6 4.7 multiply_convert_fusion.2
  89.4 0.0 copy-start.2
  89.4 0.0 copy-start.4
  89.4 0.8 copy-done.2
  90.2 0.2 copy-done.4
  90.4 1.1 pad_maximum_fusion
  91.5 0.0 all-gather.2.cloned.1.call-update
  91.5 0.0 copy-start.3
  91.5 0.0 copy-start.7
  91.5 2.7 fusion.2
  94.2 1.4 fusion.20
  95.7 2.4 copy.106
  98.1 0.5 broadcast.74
  98.6 11.3 %reduce.1 = bf16[384,2048]{1,0:T(8,128)(2,1)} reduce(bf16[384,1,2048]{2,1,0:T(2,128)(2,1)S(1)} %bitcast.98, bf16[]{:T(256)} %broadcast.74), dimensions={1}, to_apply=%bitcast.97.reduce_sub_computation | reduce | bytes 3145730
  109.9 4.2 reshape.180
  114.1 5.2 %all-to-all-start.2 = ((bf16[4,2,98304]{2,1,0:T(2,128)(2,1)}), bf16[4,2,98304]{2,1,0:T(2,128)(2,1)S(1)}, u32[]{:S(2)}, u32[]{:S(2)}) async-start(bf16[4,2,98304]{2,1,0:T(2,128)(2,1)} %reshape.180), calls=%async_computation.2 | async-start | bytes 3145728 | tf_op jit(solution)/shard_map/all_to_all | solution.py:67
  119.2 2.0 copy.97
  121.3 1.5 copy.90
  122.7 14.9 %all-to-all-done.2 = bf16[4,2,98304]{2,1,0:T(2,128)(2,1)S(1)} async-done(((bf16[4,2,98304]{2,1,0:T(2,128)(2,1)}), bf16[4,2,98304]{2,1,0:T(2,128)(2,1)S(1)}, u32[]{:S(2)}, u32[]{:S(2)}) %all-to-all-start.2) | async-done | bytes 1572896 | tf_op jit(solution)/shard_map/all_to_all | solution.py:67
  137.7 6.1 %all-to-all-start.3 = ((bf16[1,384,8,256]{3,1,0,2:T(8,128)(2,1)}), bf16[1,384,8,256]{3,1,0,2:T(8,128)(2,1)}, u32[]{:S(2)}, u32[]{:S(2)}) async-start(bf16[1,384,8,256]{3,1,0,2:T(8,128)(2,1)} %copy.90), calls=%async_computation.3 | async-start | bytes 3145728 | tf_op jit(solution)/shard_map/all_to_all | solution.py:77
  143.8 0.6 dynamic-slice
  145.0 2.9 reshape.181
  147.9 4.0 fusion.26
  151.9 165.5 %all-reduce.3.cloned.1.call-done = f32[768,1,2048]{2,1,0:T(1,128)} async-done(((f32[768,1,2048]{2,1,0:T(1,128)}), f32[768,1,2048]{2,1,0:T(1,128)}) %all-reduce.3.cloned.1.call-update) | async-done | bytes 6291472
  317.5 1.2 dynamic-slice_bitcast_fusion
  318.6 1.1 copy.94
  319.8 0.0 all-to-all-done.3
  319.8 137.6 %all-gather.2.cloned.1.call-done = bf16[1,3072,1536]{2,1,0:T(8,128)(2,1)} async-done(((bf16[1,384,1536]{2,1,0:T(8,128)(2,1)}), bf16[1,3072,1536]{2,1,0:T(8,128)(2,1)}) %all-gather.2.cloned.1.call-update) | async-done | bytes 9437200 | tf_op jit(solution)/shard_map/all_gather | solution.py:83
  457.4 5.7 %fusion.17 = f32[256,1,1536]{0,2,1:T(8,128)S(1)} fusion(bf16[3072,256]{1,0:T(8,128)(2,1)} %bitcast.16, bf16[1,3072,1536]{2,1,0:T(8,128)(2,1)} %all-gather.2.cloned.1.call-done), kind=kOutput, calls=%fused_computation.17 | convolution fusion | flops 2416312320 | bytes 12582912 | tf_op jit(solution)/shard_map/erc,erj->cej/dot_general | solution.py:80
  463.1 1.2 slice_bitcast_fusion
  464.4 2.4 copy.92
  466.8 2.3 copy.93
  (15 shorter events, 0.1 us)
Async XLA Ops:
  7.2 36.1 %copy-start = (bf16[1,2048,768]{2,1,0:T(8,128)(2,1)S(1)}, bf16[1,2048,768]{2,1,0:T(8,128)(2,1)}, u32[]{:S(2)}) copy-start(bf16[1,2048,768]{2,1,0:T(8,128)(2,1)} %param.11) | copy-start | bytes 9437188
  13.9 23.3 %all-to-all-start.1 = ((bf16[4,96,2048]{2,1,0:T(8,128)(2,1)}), bf16[4,96,2048]{2,1,0:T(8,128)(2,1)}, u32[]{:S(2)}, u32[]{:S(2)}) async-start(bf16[4,96,2048]{2,1,0:T(8,128)(2,1)} %bitcast.99), calls=%async_computation.1 | async-start | bytes 3145728 | tf_op jit(solution)/shard_map/all_to_all | solution.py:62
  22.1 3.7 copy-start.5
  37.2 24.5 %all-to-all-start = ((bf16[4,96,2048]{2,1,0:T(8,128)(2,1)}), bf16[4,96,2048]{2,1,0:T(8,128)(2,1)}, u32[]{:S(2)}, u32[]{:S(2)}) async-start(bf16[4,96,2048]{2,1,0:T(8,128)(2,1)} %bitcast.100), calls=%async_computation | async-start | bytes 3145728 | tf_op jit(solution)/shard_map/all_to_all | solution.py:63
  43.2 274.2 %all-reduce.3.cloned.1.call-start = ((), (), s32[]{:S(2)}) async-start(), calls=%async_computation.5 | async-start | bytes 12582912
  43.2 4.1 copy-start.6
  84.4 373.0 %all-gather.2.cloned.1.call-start = ((), (), s32[]{:S(2)}) async-start(), calls=%async_computation.4 | async-start | bytes 10616832 | tf_op jit(solution)/shard_map/all_gather | solution.py:83
  89.4 0.8 copy-start.2
  89.4 1.0 copy-start.4
  91.5 2.7 copy-start.3
  91.5 2.7 copy-start.7
  114.1 23.6 %all-to-all-start.2 = ((bf16[4,2,98304]{2,1,0:T(2,128)(2,1)}), bf16[4,2,98304]{2,1,0:T(2,128)(2,1)S(1)}, u32[]{:S(2)}, u32[]{:S(2)}) async-start(bf16[4,2,98304]{2,1,0:T(2,128)(2,1)} %reshape.180), calls=%async_computation.2 | async-start | bytes 3145728 | tf_op jit(solution)/shard_map/all_to_all | solution.py:67
  122.7 21.1 %copy-start.8 = (u32[32]{0:T(128)S(1)}, u32[32]{0:T(128)}, u32[]{:S(2)}) copy-start(u32[32]{0:T(128)} %constant.25) | copy-start | bytes 388
  137.7 182.1 %all-to-all-start.3 = ((bf16[1,384,8,256]{3,1,0,2:T(8,128)(2,1)}), bf16[1,384,8,256]{3,1,0,2:T(8,128)(2,1)}, u32[]{:S(2)}, u32[]{:S(2)}) async-start(bf16[1,384,8,256]{3,1,0,2:T(8,128)(2,1)} %copy.90), calls=%async_computation.3 | async-start | bytes 3145728 | tf_op jit(solution)/shard_map/all_to_all | solution.py:77
  464.4 4.7 copy-start.1
Sparse Core Ops, SparseCore 0:
  84.5 232.8 all-reduce.2
  319.9 137.4 all-gather.1
where the time goes:
time: 480 us; the launch traced here: 476 us
  waiting for transfers between devices  336 us (70%)
  local copies, waits for them, and re-layouts  48.3 us (10%)
  matrix products  39.4 us (8%)
  starting transfers between devices  22.3 us (5%)
  between operations  14.9 us (3%)
  other arithmetic  14.6 us (3%)
    unnamed x3, waiting for transfers between devices  166 us
    all_gather x1, waiting for transfers between devices, body(): lax.all_gather(stacked, 'dp', axis=1, tiled=True)  138 us
    unnamed x27, local copies, waits for them, and re-layouts  18 us
    mul x1, local copies, waits for them, and re-layouts, body(): jnp.einsum('erc,erd->ced', hidden, scaled, preferred_element_type=jnp.flo...  15.9 us
    all_to_all x1, waiting for transfers between devices, body(): lax.all_to_all(route_grad, 'expert', split_axis=1, concat_axis=0, tiled=T...  14.9 us
    unnamed x2, other arithmetic  11.4 us
    all_to_all x1, waiting for transfers between devices, body(): lax.all_to_all(send_scaled, 'expert', split_axis=0, concat_axis=1, tiled=...  10.6 us
  transfers between devices with their start and end apart: 6, of which 5 were waited for; matrix products, arithmetic and copies ran while one was open for 13% of the time, Pallas kernels for 0%

commit v1 on v0

v1 whole, which is shorter than its diff:
```python
import functools

import jax
import jax.numpy as jnp
from jax import lax
from jax.experimental import pallas as pl
from jax.experimental.pallas import tpu as pltpu
from jax.sharding import PartitionSpec as P

MESH = pl.DeviceIdType.MESH
BF16 = jnp.bfloat16
F32 = jnp.float32


def greet(targets):
    barrier = pltpu.get_barrier_semaphore()
    for target in targets:
        pl.semaphore_signal(barrier, inc=1, device_id=target, device_id_type=MESH)
    pl.semaphore_wait(barrier, len(targets))


def dispatch_kernel(
    span, parts, x_ref, g_ref, c_ref, xs_ref, gs_ref, cs_ref,
    own_sem, core_send, core_recv, chip_send, chip_recv, fwd_send, fwd_recv, c_send, c_recv,
):
    me = lax.axis_index("expert")
    core = lax.rem(me, 2)
    chip = me // 2
    other = chip * 2 + (1 - core)
    chips = span // 2
    greet([{"expert": lax.rem(me + step, span)} for step in range(1, span)])
    rows = x_ref.shape[0] // parts

    def piece(ref, part):
        return ref.at[pl.ds(part * rows, rows)]

    pairs = ((x_ref, xs_ref), (g_ref, gs_ref))
    started, locals_, forwards = [], [], []
    for step in range(1, span):
        copy = pltpu.make_async_remote_copy(
            src_ref=c_ref, dst_ref=cs_ref.at[me], send_sem=c_send.at[step], recv_sem=c_recv.at[step],
            device_id={"expert": lax.rem(me + step, span)}, device_id_type=MESH,
        )
        copy.start()
        started.append(copy)
    chip_copies = []
    for array, (source, target) in enumerate(pairs):
        for part in range(parts):
            for step in range(1, chips):
                there = lax.rem(chip + step, chips) * 2 + core
                copy = pltpu.make_async_remote_copy(
                    src_ref=piece(source, part), dst_ref=piece(target.at[me], part),
                    send_sem=chip_send.at[array, part, step], recv_sem=chip_recv.at[array, part, step],
                    device_id={"expert": there}, device_id_type=MESH,
                )
                copy.start()
                chip_copies.append((array, part, step, copy))
    for array, (source, target) in enumerate(pairs):
        copy = pltpu.make_async_remote_copy(
            src_ref=source, dst_ref=target.at[me], send_sem=core_send.at[array], recv_sem=core_recv.at[array],
            device_id={"expert": other}, device_id_type=MESH,
        )
        copy.start()
        started.append(copy)
        mine = pltpu.make_async_copy(source, target.at[me], own_sem.at[array])
        mine.start()
        locals_.append(mine)
    mine = pltpu.make_async_copy(c_ref, cs_ref.at[me], own_sem.at[2])
    mine.start()
    locals_.append(mine)
    for array, part, step, copy in chip_copies:
        copy.wait_recv()
        owner = lax.rem(chip + chips - step, chips) * 2 + core
        block = piece(pairs[array][1].at[owner], part)
        forward = pltpu.make_async_remote_copy(
            src_ref=block, dst_ref=block,
            send_sem=fwd_send.at[array, part, step], recv_sem=fwd_recv.at[array, part, step],
            device_id={"expert": other}, device_id_type=MESH,
        )
        forward.start()
        forwards.append(forward)
    for copy in locals_:
        copy.wait()
    for _, _, _, copy in chip_copies:
        copy.wait_send()
    for copy in started + forwards:
        copy.wait()


def dispatch(tokens, d_out, coef, span):
    parts = 4
    rows, width = tokens.shape
    lanes = coef.shape[1]
    dma = pltpu.SemaphoreType.DMA
    chips = span // 2
    whole = pl.BlockSpec(memory_space=pltpu.VMEM)
    return pl.pallas_call(
        functools.partial(dispatch_kernel, span, parts),
        out_shape=(
            jax.ShapeDtypeStruct((span, rows, width), BF16),
            jax.ShapeDtypeStruct((span, rows, width), BF16),
            jax.ShapeDtypeStruct((span, rows, lanes), F32),
        ),
        in_specs=[whole] * 3,
        out_specs=[whole] * 3,
        scratch_shapes=[
            dma((3,)), dma((2,)), dma((2,)), dma((2, parts, chips)), dma((2, parts, chips)),
            dma((2, parts, chips)), dma((2, parts, chips)), dma((span,)), dma((span,)),
        ],
        compiler_params=pltpu.CompilerParams(
            collective_id=0, has_side_effects=True, vmem_limit_bytes=40 << 20
        ),
        name="dispatch",
    )(tokens, d_out, coef)


def reduce_kernel(
    span, replicas, gate_ref, up_ref, down_ref, route_ref, gate_out, up_out, down_out, tok_out,
    near_a, near_b, near_c, sum_a, sum_b, sum_c, far_a, far_b, far_c, back,
    near_send, near_recv, far_send, far_recv, back_send, back_recv,
):
    expert = lax.axis_index("expert")
    me = lax.axis_index("dp")
    outer = replicas // 2
    side = lax.rem(me, 2)
    line = me // 2
    grads = (gate_ref, up_ref, down_ref)
    nears = (near_a, near_b, near_c)
    sums = (sum_a, sum_b, sum_c)
    fars = (far_a, far_b, far_c)
    outs = (gate_out, up_out, down_out)
    partner = line * 2 + (1 - side)

    greet(
        [{"expert": lax.rem(expert + step, span)} for step in range(1, span)]
        + [{"dp": partner}]
        + [{"dp": lax.rem(line + step, outer) * 2 + side} for step in range(1, outer)]
    )

    order = [(outer // 2 + k) for k in range(outer - outer // 2)] + list(range(1, outer // 2)) + [0]

    near_copies, far_copies, back_copies = {}, [], []
    for step in order:
        there = lax.rem(line + step, outer)
        for t in range(3):
            copy = pltpu.make_async_remote_copy(
                src_ref=grads[t].at[there * 2 + (1 - side)], dst_ref=nears[t].at[step],
                send_sem=near_send.at[t, step], recv_sem=near_recv.at[t, step],
                device_id={"dp": partner}, device_id_type=MESH,
            )
            copy.start()
            near_copies[t, step] = copy
    for step in range(1, span):
        there = lax.rem(expert + step, span)
        copy = pltpu.make_async_remote_copy(
            src_ref=route_ref.at[there], dst_ref=back.at[step],
            send_sem=back_send.at[step], recv_sem=back_recv.at[step],
            device_id={"expert": there}, device_id_type=MESH,
        )
        copy.start()
        back_copies.append(copy)
    for step in order[:-1]:
        there = lax.rem(line + step, outer)
        for t in range(3):
            near_copies[t, step].wait_recv()
            sums[t][step] = (
                grads[t][there * 2 + side].astype(F32) + nears[t][step].astype(F32)
            ).astype(BF16)
            copy = pltpu.make_async_remote_copy(
                src_ref=sums[t].at[step], dst_ref=fars[t].at[step],
                send_sem=far_send.at[t, step], recv_sem=far_recv.at[t, step],
                device_id={"dp": there * 2 + side}, device_id_type=MESH,
            )
            copy.start()
            far_copies.append(copy)
    for copy in back_copies:
        copy.wait_recv()
    total = route_ref[expert].astype(F32)
    for step in range(1, span):
        total = total + back[step].astype(F32)
    tok_out[...] = total.astype(BF16)
    for t in range(3):
        near_copies[t, 0].wait_recv()
        outs[t][...] = grads[t][line * 2 + side].astype(F32) + nears[t][0].astype(F32)
    at = 0
    for step in order[:-1]:
        for t in range(3):
            far_copies[at].wait_recv()
            at += 1
            outs[t][...] += fars[t][step].astype(F32)
    for copy in list(near_copies.values()) + far_copies + back_copies:
        copy.wait_send()


def reduce_return(grad_gate, grad_up, grad_down, route_grad, span, replicas):
    outer = replicas // 2
    dma = pltpu.SemaphoreType.DMA
    whole = pl.BlockSpec(memory_space=pltpu.VMEM)
    shards = [g.shape[1:] for g in (grad_gate, grad_up, grad_down)]
    slots = [pltpu.VMEM((outer,) + s, BF16) for s in shards]
    rows, width = route_grad.shape[1:]
    return pl.pallas_call(
        functools.partial(reduce_kernel, span, replicas),
        out_shape=tuple(jax.ShapeDtypeStruct(s, F32) for s in shards)
        + (jax.ShapeDtypeStruct((rows, width), BF16),),
        in_specs=[whole] * 4,
        out_specs=[whole] * 4,
        scratch_shapes=slots * 3
        + [pltpu.VMEM((span, rows, width), BF16)]
        + [dma((3, outer)), dma((3, outer)), dma((3, outer)), dma((3, outer)), dma((span,)), dma((span,))],
        compiler_params=pltpu.CompilerParams(
            collective_id=1, has_side_effects=True, vmem_limit_bytes=56 << 20
        ),
        name="reduce_return",
    )(grad_gate, grad_up, grad_down, route_grad)


def body(tokens, d_out, routes, gate_fixed, w_gate, w_up, w_down):
    span = lax.axis_size("expert")
    replicas = lax.axis_size("dp")
    me = lax.axis_index("expert")
    rows, width = tokens.shape
    hidden_units = w_gate.shape[2]
    w_gate, w_up, w_down = w_gate[0], w_up[0], w_down[0]
    lanes = jnp.arange(128, dtype=jnp.int32)
    gate_value = gate_fixed.astype(F32) / 65536.0
    coef = jnp.sum(
        jnp.where(routes[:, :, None] == lanes[None, None, :], gate_value[:, :, None], 0.0), axis=1
    )
    xs, gs, cs = dispatch(tokens, d_out, coef, span)
    x = xs.reshape(span * rows, width)
    weight = jnp.sum(
        jnp.where(lanes[None, :] == me, cs.reshape(span * rows, 128), 0.0), axis=1, keepdims=True
    )
    scaled = (weight * gs.reshape(span * rows, width).astype(F32)).astype(BF16)
    pre_gate = jnp.dot(x, w_gate, preferred_element_type=F32)
    pre_up = jnp.dot(x, w_up, preferred_element_type=F32)
    sigmoid_gate = jax.nn.sigmoid(pre_gate)
    silu_gate = pre_gate * sigmoid_gate
    hidden = (silu_gate * pre_up).astype(BF16)
    d_hidden = lax.dot_general(scaled, w_down, (((1,), (1,)), ((), ())), preferred_element_type=F32)
    d_gate = (d_hidden * pre_up * sigmoid_gate * (1.0 + pre_gate * (1.0 - sigmoid_gate))).astype(BF16)
    d_up = (d_hidden * silu_gate).astype(BF16)
    route_grad = (
        lax.dot_general(d_gate, w_gate, (((1,), (1,)), ((), ())), preferred_element_type=F32)
        + lax.dot_general(d_up, w_up, (((1,), (1,)), ((), ())), preferred_element_type=F32)
    ).astype(BF16)

    def outer_product(left, right):
        return lax.dot_general(
            left, right, (((0,), (0,)), ((), ())), preferred_element_type=F32
        ).astype(BF16)

    grad_gate = outer_product(x, d_gate).reshape(replicas, width // replicas, hidden_units)
    grad_up = outer_product(x, d_up).reshape(replicas, width // replicas, hidden_units)
    grad_down = outer_product(hidden, scaled).reshape(replicas, hidden_units // replicas, width)
    out_gate, out_up, out_down, d_tokens = reduce_return(
        grad_gate, grad_up, grad_down, route_grad.reshape(span, rows, width), span, replicas
    )
    inverse = 1.0 / replicas
    return (d_tokens, (out_gate * inverse)[None], (out_up * inverse)[None], (out_down * inverse)[None])


def solution(mesh):
    rows = P(("dp", "expert"), None)
    whole = P("expert", None, None)
    cut = P("expert", "dp", None)
    return jax.shard_map(
        body, mesh=mesh, in_specs=(rows,) * 4 + (whole,) * 3, out_specs=(rows, cut, cut, cut), check_vma=False
    )
```

time: 480 us -> 187 us (0.39)
  waiting for transfers between devices: 336 us -> 0 us
  Pallas kernels: 0 us -> 152 us
  local copies, waits for them, and re-layouts: 48.3 us -> 4.46 us
  starting transfers between devices: 22.3 us -> 0 us
  matrix products: 39.4 us -> 21.5 us
  between operations: 14.9 us -> 0.77 us
  other arithmetic: 14.6 us -> 6.16 us
    unnamed x3 -> x0, waiting for transfers between devices: 166 us -> none
    pallas_call x0 -> x2, Pallas kernels: none -> 152 us  [the longest x1 122 us: reduce_return(): pl.pallas_call(functools.partial(reduce_kernel, span, replicas), out_shap...]
    all_gather x1 -> x0, waiting for transfers between devices: 138 us -> none  [body(): lax.all_gather(stacked, 'dp', axis=1, tiled=True)]
    all_to_all x4 -> x0, waiting for transfers between devices: 33.2 us -> none  [the longest x1 14.9 us: body(): lax.all_to_all(route_grad, 'expert', split_axis=1, concat_axis=0, tiled=T...]
    mul x4 -> x0, local copies, waits for them, and re-layouts: 23.2 us -> none  [the longest x1 15.9 us: body(): jnp.einsum('erc,erd->ced', hidden, scaled, preferred_element_type=jnp.flo...]
    all_to_all x4 -> x0, starting transfers between devices: 22.1 us -> none  [the longest x1 6.14 us: body(): lax.all_to_all(split_rows, 'dp', split_axis=2, concat_axis=1, tiled=True)]
    dot_general x10 -> x8, matrix products: 39.4 us -> 21.5 us  [the longest x3 10.6 us: outer_product(): lax.dot_general(left, right, (((0,), (0,)), ((), ())), preferred_element_...]
    unnamed x27 -> x17, local copies, waits for them, and re-layouts: 18 us -> 4.46 us
  transfers between devices with their start and end apart: 6 -> 0, of which waited for: 5 -> 0; matrix products, arithmetic and copies ran while one was open for 13% -> 0% of each run, Pallas kernels for 0% -> 0%
where the time goes in v1:
time: 187 us; the launch traced here: 185 us
  Pallas kernels  152 us (81%)
  matrix products  21.5 us (11%)
  other arithmetic  6.16 us (3%)
  local copies, waits for them, and re-layouts  4.46 us (2%)
    pallas_call x1, Pallas kernels, reduce_return(): pl.pallas_call(functools.partial(reduce_kernel, span, replicas), out_shap...  122 us
    pallas_call x1, Pallas kernels, dispatch(): pl.pallas_call(functools.partial(dispatch_kernel, span, parts), out_shape...  30 us
    dot_general x3, matrix products, outer_product(): lax.dot_general(left, right, (((0,), (0,)), ((), ())), preferred_element_...  10.6 us
    unnamed x17, local copies, waits for them, and re-layouts  4.46 us

profile of v1, /device:TPU:20, one launch (start us, length us, event | category | flops | bytes accessed | tf_op | source)
XLA Modules:
  0.0 185.1 jit_solution(856593021646399164)
XLA Ops:
  0.6 0.0 copy-start
  0.7 0.8 convert_multiply_fusion
  1.5 0.9 select_reduce_fusion.1.c_ref
  2.4 0.0 copy-start.1
  2.4 1.0 copy-done.1
  3.5 0.0 copy-start.2
  3.5 1.0 copy-done.2
  4.5 30.0 %dispatch.1 = (bf16[4,128,2048]{2,1,0:T(8,128)(2,1)S(1)}, bf16[4,128,2048]{2,1,0:T(8,128)(2,1)S(1)}, f32[4,128,128]{2,1,0:T(8,128)S(1)}) custom-call(bf16[128,2048]{1,0:T(8,128)(2,1)S(1)} %copy-done.1, bf16[128,2048]{1,0:T(8,128)(2,1)S(1)} %copy-done.2, f32[128,128]{1,0:T(8,128)S(1)} %select_reduce_fusion.1.c_ref), custom_call_target="tpu_custom_call" | custom-call | tf_op jit(solution)/shard_map/dispatch/pallas_call | solution.py:97
  34.5 0.1 select_reduce_fusion
  34.6 0.0 copy-done
  34.7 0.0 copy-start.7
  34.7 1.8 fusion.3
  36.5 0.1 copy-done.7
  36.5 1.8 fusion.7
  38.3 0.4 fusion
  38.8 0.0 copy-start.6
  38.8 0.4 multiply_convert_fusion
  39.2 1.5 copy-done.6
  40.6 2.2 %multiply_convert_fusion.2 = (bf16[512,768]{1,0:T(8,128)(2,1)S(1)}, bf16[512,768]{1,0:T(8,128)(2,1)S(1)}) fusion(f32[512,768]{1,0:T(8,128)S(1)} %fusion.3, f32[512,768]{1,0:T(8,128)S(1)} %fusion.7, bf16[512,2048]{1,0:T(8,128)(2,1)S(1)} %bitcast.51, bf16[1,768,2048]{2,1,0:T(8,128)(2,1)S(1)} %copy-done.6), kind=kOutput, calls=%fused_computation.18 | convolution fusion | flops 1615724544 | bytes 9961472 | tf_op jit(solution)/shard_map/dot_general | solution.py:241
  42.9 3.6 %convolution_convert_fusion = bf16[768,2048]{1,0:T(8,128)(2,1)} fusion(bf16[512,2048]{1,0:T(8,128)(2,1)S(1)} %fusion, f32[512,768]{1,0:T(8,128)S(1)} %fusion.7, f32[512,768]{1,0:T(8,128)S(1)} %fusion.3), kind=kOutput, calls=%fused_computation.4 | convolution fusion | flops 1614544896 | bytes 8388608 | tf_op jit(solution)/shard_map/dot_general | solution.py:250
  46.4 3.5 %convolution_convert_fusion.1 = bf16[2048,768]{1,0:T(8,128)(2,1)} fusion(bf16[512,2048]{1,0:T(8,128)(2,1)S(1)} %bitcast.46, bf16[512,768]{1,0:T(8,128)(2,1)S(1)} %get-tuple-element.18), kind=kOutput, calls=%fused_computation.5 | convolution fusion | flops 1612185600 | bytes 6029312 | tf_op jit(solution)/shard_map/dot_general | solution.py:250
  50.0 3.5 %convolution_convert_fusion.2 = bf16[2048,768]{1,0:T(8,128)(2,1)} fusion(bf16[512,2048]{1,0:T(8,128)(2,1)S(1)} %bitcast.47, bf16[512,768]{1,0:T(8,128)(2,1)S(1)} %get-tuple-element.19), kind=kOutput, calls=%fused_computation.6 | convolution fusion | flops 1612185600 | bytes 6029312 | tf_op jit(solution)/shard_map/dot_general | solution.py:250
  53.5 2.0 %fusion.1 = f32[512,2048]{1,0:T(8,128)S(1)} fusion(bf16[512,768]{1,0:T(8,128)(2,1)S(1)} %get-tuple-element.19, bf16[1,2048,768]{2,1,0:T(8,128)(2,1)S(1)} %copy-done), kind=kOutput, calls=%fused_computation.7 | convolution fusion | flops 1610612736 | bytes 8126464 | tf_op jit(solution)/shard_map/dot_general | solution.py:245
  55.5 3.1 %add_convert_fusion = bf16[512,2048]{1,0:T(8,128)(2,1)} fusion(f32[512,2048]{1,0:T(8,128)S(1)} %fusion.1, bf16[512,768]{1,0:T(8,128)(2,1)S(1)} %get-tuple-element.18, bf16[1,2048,768]{2,1,0:T(8,128)(2,1)S(1)} %copy-done.7), kind=kOutput, calls=%fused_computation.2 | convolution fusion | flops 1612709888 | bytes 10223616 | tf_op jit(solution)/shard_map/dot_general | solution.py:246
  58.6 122.1 %reduce_return.1 = (f32[256,768]{1,0:T(8,128)}, f32[256,768]{1,0:T(8,128)}, f32[96,2048]{1,0:T(8,128)}, bf16[128,2048]{1,0:T(8,128)(2,1)}) custom-call(bf16[8,256,768]{2,1,0:T(8,128)(2,1)} %bitcast.50, bf16[8,256,768]{2,1,0:T(8,128)(2,1)} %bitcast.49, bf16[8,96,2048]{2,1,0:T(8,128)(2,1)} %bitcast.48, bf16[4,128,2048]{2,1,0:T(8,128)(2,1)} %bitcast.52), custom_call_target="tpu_custom_call" | custom-call | tf_op jit(solution)/shard_map/reduce_return/pallas_call | solution.py:202
  180.8 0.0 copy-start.3
  180.8 0.0 copy-start.4
  180.8 0.0 copy-start.5
  180.8 2.2 %multiply_bitcast_fusion = f32[1,96,2048]{2,1,0:T(8,128)} fusion(f32[96,2048]{1,0:T(8,128)} %get-tuple-element.17), kind=kLoop, calls=%fused_computation.22 | loop fusion | flops 196608 | bytes 1572864 | tf_op jit(solution)/shard_map/broadcast_in_dim | solution.py:261
  183.0 0.0 copy-done.3
  183.0 0.0 copy-done.4
  183.0 1.2 multiply_bitcast_fusion.1
  184.3 0.0 copy-done.5
  184.3 0.8 copy.14
  (1 shorter events, 0.0 us)
Async XLA Ops:
  0.6 34.0 %copy-start = (bf16[1,2048,768]{2,1,0:T(8,128)(2,1)S(1)}, bf16[1,2048,768]{2,1,0:T(8,128)(2,1)}, u32[]{:S(2)}) copy-start(bf16[1,2048,768]{2,1,0:T(8,128)(2,1)} %param.11) | copy-start | bytes 9437188
  2.4 1.0 copy-start.1
  3.5 1.0 copy-start.2
  34.7 1.9 %copy-start.7 = (bf16[1,2048,768]{2,1,0:T(8,128)(2,1)S(1)}, bf16[1,2048,768]{2,1,0:T(8,128)(2,1)}, u32[]{:S(2)}) copy-start(bf16[1,2048,768]{2,1,0:T(8,128)(2,1)} %param.12) | copy-start | bytes 9437188
  38.8 1.9 %copy-start.6 = (bf16[1,768,2048]{2,1,0:T(8,128)(2,1)S(1)}, bf16[1,768,2048]{2,1,0:T(8,128)(2,1)}, u32[]{:S(2)}) copy-start(bf16[1,768,2048]{2,1,0:T(8,128)(2,1)} %param.13) | copy-start | bytes 9437188
  180.8 2.3 %copy-start.3 = (f32[256,768]{1,0:T(8,128)S(1)}, f32[256,768]{1,0:T(8,128)}, u32[]{:S(2)}) copy-start(f32[256,768]{1,0:T(8,128)} %get-tuple-element.15) | copy-start | bytes 2359300
  180.8 2.2 %copy-start.4 = (f32[256,768]{1,0:T(8,128)S(1)}, f32[256,768]{1,0:T(8,128)}, u32[]{:S(2)}) copy-start(f32[256,768]{1,0:T(8,128)} %get-tuple-element.16) | copy-start | bytes 2359300
  180.8 3.5 %copy-start.5 = (bf16[128,2048]{1,0:T(8,128)(2,1)S(1)}, bf16[128,2048]{1,0:T(8,128)(2,1)}, u32[]{:S(2)}) copy-start(bf16[128,2048]{1,0:T(8,128)(2,1)} %get-tuple-element.26) | copy-start | bytes 1572868

commit v2 on v1

v2 whole, which is shorter than its diff:
```python
import functools

import jax
import jax.numpy as jnp
from jax import lax
from jax.experimental import pallas as pl
from jax.experimental.pallas import tpu as pltpu
from jax.sharding import PartitionSpec as P

MESH = pl.DeviceIdType.MESH
BF16 = jnp.bfloat16
F32 = jnp.float32


def greet(targets):
    barrier = pltpu.get_barrier_semaphore()
    for target in targets:
        pl.semaphore_signal(barrier, inc=1, device_id=target, device_id_type=MESH)
    pl.semaphore_wait(barrier, len(targets))


def dispatch_kernel(
    span, parts, x_ref, g_ref, c_ref, xs_ref, gs_ref, cs_ref,
    own_sem, core_send, core_recv, chip_send, chip_recv, fwd_send, fwd_recv, c_send, c_recv,
):
    me = lax.axis_index("expert")
    core = lax.rem(me, 2)
    chip = me // 2
    other = chip * 2 + (1 - core)
    chips = span // 2
    greet([{"expert": lax.rem(me + step, span)} for step in range(1, span)])
    rows = x_ref.shape[0] // parts

    def piece(ref, part):
        return ref.at[pl.ds(part * rows, rows)]

    pairs = ((x_ref, xs_ref), (g_ref, gs_ref))
    started, locals_, forwards = [], [], []
    for step in range(1, span):
        copy = pltpu.make_async_remote_copy(
            src_ref=c_ref, dst_ref=cs_ref.at[me], send_sem=c_send.at[step], recv_sem=c_recv.at[step],
            device_id={"expert": lax.rem(me + step, span)}, device_id_type=MESH,
        )
        copy.start()
        started.append(copy)
    chip_copies = []
    for array, (source, target) in enumerate(pairs):
        for part in range(parts):
            for step in range(1, chips):
                there = lax.rem(chip + step, chips) * 2 + core
                copy = pltpu.make_async_remote_copy(
                    src_ref=piece(source, part), dst_ref=piece(target.at[me], part),
                    send_sem=chip_send.at[array, part, step], recv_sem=chip_recv.at[array, part, step],
                    device_id={"expert": there}, device_id_type=MESH,
                )
                copy.start()
                chip_copies.append((array, part, step, copy))
    for array, (source, target) in enumerate(pairs):
        copy = pltpu.make_async_remote_copy(
            src_ref=source, dst_ref=target.at[me], send_sem=core_send.at[array], recv_sem=core_recv.at[array],
            device_id={"expert": other}, device_id_type=MESH,
        )
        copy.start()
        started.append(copy)
        mine = pltpu.make_async_copy(source, target.at[me], own_sem.at[array])
        mine.start()
        locals_.append(mine)
    mine = pltpu.make_async_copy(c_ref, cs_ref.at[me], own_sem.at[2])
    mine.start()
    locals_.append(mine)
    for array, part, step, copy in chip_copies:
        copy.wait_recv()
        owner = lax.rem(chip + chips - step, chips) * 2 + core
        block = piece(pairs[array][1].at[owner], part)
        forward = pltpu.make_async_remote_copy(
            src_ref=block, dst_ref=block,
            send_sem=fwd_send.at[array, part, step], recv_sem=fwd_recv.at[array, part, step],
            device_id={"expert": other}, device_id_type=MESH,
        )
        forward.start()
        forwards.append(forward)
    for copy in locals_:
        copy.wait()
    for _, _, _, copy in chip_copies:
        copy.wait_send()
    for copy in started + forwards:
        copy.wait()


def dispatch(tokens, d_out, coef, span):
    parts = 4
    rows, width = tokens.shape
    dma = pltpu.SemaphoreType.DMA
    chips = span // 2
    whole = pl.BlockSpec(memory_space=pltpu.VMEM)
    return pl.pallas_call(
        functools.partial(dispatch_kernel, span, parts),
        out_shape=(
            jax.ShapeDtypeStruct((span, rows, width), BF16),
            jax.ShapeDtypeStruct((span, rows, width), BF16),
            jax.ShapeDtypeStruct((span,) + coef.shape, F32),
        ),
        in_specs=[whole] * 3,
        out_specs=[whole] * 3,
        scratch_shapes=[
            dma((3,)), dma((2,)), dma((2,)), dma((2, parts, chips)), dma((2, parts, chips)),
            dma((2, parts, chips)), dma((2, parts, chips)), dma((span,)), dma((span,)),
        ],
        compiler_params=pltpu.CompilerParams(
            collective_id=0, has_side_effects=True, vmem_limit_bytes=40 << 20
        ),
        name="dispatch",
    )(tokens, d_out, coef)


def reduce_kernel(
    span, replicas, x_ref, scaled_ref, hidden_ref, dg_ref, du_ref, wg_ref, wu_ref,
    gate_out, up_out, down_out, tok_out,
    grad_a, grad_b, grad_c, near_a, near_b, near_c, sum_a, sum_b, sum_c, line_a, line_b, line_c, route, back,
    near_send, near_recv, line_send, line_recv, back_send, back_recv,
):
    expert = lax.axis_index("expert")
    me = lax.axis_index("dp")
    outer = replicas // 2
    side = lax.rem(me, 2)
    line = me // 2
    partner = line * 2 + (1 - side)
    grads = (grad_a, grad_b, grad_c)
    nears = (near_a, near_b, near_c)
    sums = (sum_a, sum_b, sum_c)
    lines = (line_a, line_b, line_c)
    outs = (gate_out, up_out, down_out)
    tensors = (2, 0, 1)
    lower = lax.rem(line + outer - 1, outer) * 2 + side
    upper = lax.rem(line + 1, outer) * 2 + side

    targets = [{"expert": lax.rem(expert + step, span)} for step in range(1, span)]
    targets += [{"dp": partner}, {"dp": lower}, {"dp": upper}]
    greet(targets)

    place = jnp.where(line < outer // 2, 2 * line + 1, 2 * (outer - 1 - line))

    def order_at(i):
        j = i + jnp.where(i >= place, 1, 0)
        half = j // 2
        d = jnp.where(lax.rem(j, 2) == 0, outer - 1 - half, half)
        return jnp.where(i == outer - 1, line, d)

    def near_copy(t, d):
        return pltpu.make_async_remote_copy(
            src_ref=grads[t].at[d * 2 + (1 - side)], dst_ref=nears[t].at[d],
            send_sem=near_send.at[t, d], recv_sem=near_recv.at[t, d],
            device_id={"dp": partner}, device_id_type=MESH,
        )

    def line_copy(t, d):
        following = jnp.where(d > line, line + 1, line - 1)
        slot = jnp.where((d < line) & (d == following), outer, d)
        return pltpu.make_async_remote_copy(
            src_ref=sums[t].at[d], dst_ref=lines[t].at[slot],
            send_sem=line_send.at[t, d], recv_sem=line_recv.at[t, slot],
            device_id={"dp": following * 2 + side}, device_id_type=MESH,
        )

    def line_wait(t, slot):
        pltpu.make_async_remote_copy(
            src_ref=lines[t].at[slot], dst_ref=lines[t].at[slot],
            send_sem=line_send.at[t, 0], recv_sem=line_recv.at[t, slot],
            device_id={"dp": upper}, device_id_type=MESH,
        ).wait_recv()

    def back_copy(step):
        there = lax.rem(expert + step, span)
        return pltpu.make_async_remote_copy(
            src_ref=route.at[step], dst_ref=back.at[step],
            send_sem=back_send.at[step], recv_sem=back_recv.at[step],
            device_id={"expert": there}, device_id_type=MESH,
        )

    def outer_product(left, right):
        return lax.dot_general(left, right, (((0,), (0,)), ((), ())), preferred_element_type=F32)

    units = hidden_ref.shape[1]
    width = units // 2
    shard = units // replicas
    for part in range(2):
        product = outer_product(hidden_ref[:, part * width : (part + 1) * width], scaled_ref[...])
        for piece in range(width // shard):
            grad_c[part * (width // shard) + piece] = product[piece * shard : (piece + 1) * shard].astype(BF16)

    def start_down(i, carry):
        near_copy(2, order_at(i)).start()
        return carry

    lax.fori_loop(0, outer, start_down, 0)
    feature = x_ref.shape[1] // replicas

    def start_pair(i, carry):
        d = order_at(i)
        columns = x_ref[:, pl.ds(pl.multiple_of(d * 2 * feature, 2 * feature), 2 * feature)]
        for t, right in ((0, dg_ref), (1, du_ref)):
            product = outer_product(columns, right[...])
            grads[t][d * 2] = product[:feature].astype(BF16)
            grads[t][d * 2 + 1] = product[feature:].astype(BF16)
            near_copy(t, d).start()
        return carry

    lax.fori_loop(0, outer, start_pair, 0)
    rows = tok_out.shape[0]

    def route_block(step):
        there = lax.rem(expert + step, span)
        at = pl.ds(pl.multiple_of(there * rows, rows), rows)
        contract = (((1,), (1,)), ((), ()))
        route[step] = (
            lax.dot_general(dg_ref[at, :], wg_ref[...], contract, preferred_element_type=F32)
            + lax.dot_general(du_ref[at, :], wu_ref[...], contract, preferred_element_type=F32)
        ).astype(BF16)

    def start_back(step, carry):
        route_block(step)
        back_copy(step).start()
        return carry

    lax.fori_loop(1, span, start_back, 0)

    def forward(i, carry):
        d = order_at(i)
        fed = ((d > line) & (line > 0)) | ((d < line) & (line < outer - 1))
        for t in tensors:
            near_copy(t, d).wait_recv()

            @pl.when(fed)
            def _():
                line_wait(t, d)
                sums[t][d] = (
                    grads[t][d * 2 + side].astype(F32) + nears[t][d].astype(F32) + lines[t][d].astype(F32)
                ).astype(BF16)

            @pl.when(jnp.logical_not(fed))
            def _():
                sums[t][d] = (grads[t][d * 2 + side].astype(F32) + nears[t][d].astype(F32)).astype(BF16)

            line_copy(t, d).start()
        return carry

    lax.fori_loop(0, outer - 1, forward, 0)
    route_block(0)
    for step in range(1, span):
        back_copy(step).wait_recv()
    total = route[0].astype(F32)
    for step in range(1, span):
        total = total + back[step].astype(F32)
    tok_out[...] = total.astype(BF16)
    for t in tensors:
        near_copy(t, line).wait_recv()
        outs[t][...] = grads[t][me].astype(F32) + nears[t][line].astype(F32)

        @pl.when(line > 0)
        def _():
            line_wait(t, line)
            outs[t][...] += lines[t][line].astype(F32)

        @pl.when(line < outer - 1)
        def _():
            line_wait(t, outer)
            outs[t][...] += lines[t][outer].astype(F32)

    def finish(i, carry):
        d = order_at(i)
        for t in range(3):
            near_copy(t, d).wait_send()

            @pl.when(i < outer - 1)
            def _():
                line_copy(t, d).wait_send()

        return carry

    lax.fori_loop(0, outer, finish, 0)
    for step in range(1, span):
        back_copy(step).wait_send()


def reduce_return(x, scaled, hidden, d_gate, d_up, w_gate, w_up, span, replicas):
    outer = replicas // 2
    dma = pltpu.SemaphoreType.DMA
    whole = pl.BlockSpec(memory_space=pltpu.VMEM)
    width, units = x.shape[1], hidden.shape[1]
    rows = x.shape[0] // span
    shards = [(width // replicas, units)] * 2 + [(units // replicas, width)]
    return pl.pallas_call(
        functools.partial(reduce_kernel, span, replicas),
        out_shape=tuple(jax.ShapeDtypeStruct(s, F32) for s in shards)
        + (jax.ShapeDtypeStruct((rows, width), BF16),),
        in_specs=[whole] * 7,
        out_specs=[whole] * 4,
        scratch_shapes=[pltpu.VMEM((replicas,) + s, BF16) for s in shards]
        + [pltpu.VMEM((outer,) + s, BF16) for s in shards] * 2
        + [pltpu.VMEM((outer + 1,) + s, BF16) for s in shards]
        + [pltpu.VMEM((span, rows, width), BF16)] * 2
        + [dma((3, outer)), dma((3, outer)), dma((3, outer)), dma((3, outer + 1)), dma((span,)), dma((span,))],
        compiler_params=pltpu.CompilerParams(
            collective_id=1, has_side_effects=True, vmem_limit_bytes=60 << 20
        ),
        name="reduce_return",
    )(x, scaled, hidden, d_gate, d_up, w_gate, w_up)


def body(tokens, d_out, routes, gate_fixed, w_gate, w_up, w_down):
    span = lax.axis_size("expert")
    replicas = lax.axis_size("dp")
    me = lax.axis_index("expert")
    rows, width = tokens.shape
    hidden_units = w_gate.shape[2]
    w_gate, w_up, w_down = w_gate[0], w_up[0], w_down[0]
    places = jnp.arange(max(8, span), dtype=jnp.int32)
    gate_value = gate_fixed.astype(F32) / 65536.0
    coef = jnp.sum(
        jnp.where(places[:, None, None] == routes[None], gate_value[None], 0.0), axis=2
    )
    xs, gs, cs = dispatch(tokens, d_out, coef, span)
    x = xs.reshape(span * rows, width)
    weight = jnp.sum(jnp.where(places[None, :, None] == me, cs, 0.0), axis=1).reshape(span * rows, 1)
    scaled = (weight * gs.reshape(span * rows, width).astype(F32)).astype(BF16)
    pre_gate = jnp.dot(x, w_gate, preferred_element_type=F32)
    pre_up = jnp.dot(x, w_up, preferred_element_type=F32)
    sigmoid_gate = jax.nn.sigmoid(pre_gate)
    silu_gate = pre_gate * sigmoid_gate
    hidden = (silu_gate * pre_up).astype(BF16)
    d_hidden = lax.dot_general(scaled, w_down, (((1,), (1,)), ((), ())), preferred_element_type=F32)
    d_gate = (d_hidden * pre_up * sigmoid_gate * (1.0 + pre_gate * (1.0 - sigmoid_gate))).astype(BF16)
    d_up = (d_hidden * silu_gate).astype(BF16)
    out_gate, out_up, out_down, d_tokens = reduce_return(
        x, scaled, hidden, d_gate, d_up, w_gate, w_up, span, replicas
    )
    inverse = 1.0 / replicas
    return (d_tokens, (out_gate * inverse)[None], (out_up * inverse)[None], (out_down * inverse)[None])


def solution(mesh):
    rows = P(("dp", "expert"), None)
    whole = P("expert", None, None)
    cut = P("expert", "dp", None)
    return jax.shard_map(
        body, mesh=mesh, in_specs=(rows,) * 4 + (whole,) * 3, out_specs=(rows, cut, cut, cut), check_vma=False
    )
```

time: 187 us -> 183 us (0.979); the launches traced: 185 us -> 179 us
  matrix products: 21.5 us -> 10 us
  Pallas kernels: 152 us -> 158 us
    dot_general x5 -> x0, matrix products: 15.8 us -> none  [the longest x3 10.6 us: outer_product(): lax.dot_general(left, right, (((0,), (0,)), ((), ())), preferred_element_...]
    pallas_call x1, Pallas kernels: 122 us -> 131 us  [reduce_return(): pl.pallas_call(functools.partial(reduce_kernel, span, replicas), out_shap...]
    pallas_call x1, Pallas kernels: 30 us -> 27.4 us  [dispatch(): pl.pallas_call(functools.partial(dispatch_kernel, span, parts), out_shape...]
    dot_general x1, matrix products: 1.78 us -> 4.4 us  [body(): pre_up = jnp.dot(x, w_up, preferred_element_type=F32)]
where the time goes in v2:
time: 183 us; the launch traced here: 179 us
  Pallas kernels  158 us (86%)
  matrix products  10 us (5%)
  other arithmetic  7.3 us (4%)
  local copies, waits for them, and re-layouts  2.91 us (2%)
    pallas_call x1, Pallas kernels, reduce_return(): pl.pallas_call(functools.partial(reduce_kernel, span, replicas), out_shap...  131 us
    pallas_call x1, Pallas kernels, dispatch(): pl.pallas_call(functools.partial(dispatch_kernel, span, parts), out_shape...  27.4 us
    dot_general x1, matrix products, body(): pre_up = jnp.dot(x, w_up, preferred_element_type=F32)  4.4 us
    dot_general x1, matrix products, body(): lax.dot_general(scaled, w_down, (((1,), (1,)), ((), ())), preferred_eleme...  3.8 us

profile of v2, /device:TPU:20, one launch (start us, length us, event | category | flops | bytes accessed | tf_op | source)
XLA Modules:
  0.0 179.1 jit_solution(5152398807235529807)
XLA Ops:
  0.6 0.0 copy-start
  0.7 0.8 convert_multiply_fusion
  1.5 0.8 select_reduce_fusion.1.c_ref
  2.3 0.0 copy-start.2
  2.3 1.0 copy-done.2
  3.3 0.0 copy-start.3
  3.3 1.0 copy-done.3
  4.4 27.4 %dispatch.1 = (bf16[4,128,2048]{2,1,0:T(8,128)(2,1)S(1)}, bf16[4,128,2048]{2,1,0:T(8,128)(2,1)S(1)}, f32[4,8,128]{2,1,0:T(8,128)S(1)}) custom-call(bf16[128,2048]{1,0:T(8,128)(2,1)S(1)} %copy-done.2, bf16[128,2048]{1,0:T(8,128)(2,1)S(1)} %copy-done.3, f32[8,128]{1,0:T(8,128)S(1)} %select_reduce_fusion.1.c_ref), custom_call_target="tpu_custom_call" | custom-call | tf_op jit(solution)/shard_map/dispatch/pallas_call | solution.py:96
  31.7 0.0 copy-start.1
  31.7 0.1 select_reduce_fusion
  31.8 0.0 copy-start.4
  31.8 4.4 %fusion.4 = f32[512,768]{1,0:T(8,128)S(1)} fusion(bf16[512,2048]{1,0:T(8,128)(2,1)S(1)} %bitcast.27, bf16[1,2048,768]{2,1,0:T(8,128)(2,1)} %param.12), kind=kOutput, calls=%fused_computation.18 | convolution fusion | flops 1610612736 | bytes 6815744 | tf_op jit(solution)/shard_map/dot_general | solution.py:327
  36.2 0.0 copy-done.1
  36.2 0.0 copy-done.4
  36.3 1.8 %fusion.6 = f32[512,768]{1,0:T(8,128)S(1)} fusion(bf16[512,2048]{1,0:T(8,128)(2,1)S(1)} %bitcast.28, bf16[1,2048,768]{2,1,0:T(8,128)(2,1)S(1)} %copy-done.4), kind=kOutput, calls=%fused_computation.20 | convolution fusion | flops 1610612736 | bytes 6815744 | tf_op jit(solution)/shard_map/dot_general | solution.py:326
  38.1 1.7 fusion.scaled_ref
  39.8 0.4 multiply_convert_fusion
  40.2 0.0 copy-done
  40.2 3.8 %multiply_convert_fusion.1 = (bf16[512,768]{1,0:T(8,128)(2,1)}, bf16[512,768]{1,0:T(8,128)(2,1)}, bf16[512,768]{1,0:T(8,128)(2,1)}) fusion(f32[512,768]{1,0:T(8,128)S(1)} %fusion.6, f32[512,768]{1,0:T(8,128)S(1)} %fusion.4, bf16[512,2048]{1,0:T(8,128)(2,1)S(1)} %bitcast.32, bf16[1,768,2048]{2,1,0:T(8,128)(2,1)S(1)} %copy-done), kind=kOutput, calls=%fused_computation.5 | convolution fusion | flops 1616510976 | bytes 10747904 | tf_op jit(solution)/shard_map/dot_general | solution.py:331
  44.0 130.8 %reduce_return.1 = (f32[256,768]{1,0:T(8,128)}, f32[256,768]{1,0:T(8,128)}, f32[96,2048]{1,0:T(8,128)}, bf16[128,2048]{1,0:T(8,128)(2,1)}) custom-call(bf16[512,2048]{1,0:T(8,128)(2,1)} %bitcast.29, bf16[512,2048]{1,0:T(8,128)(2,1)} %fusion.scaled_ref, bf16[512,768]{1,0:T(8,128)(2,1)} %get-tuple-element.20.hidden_ref, ...), custom_call_target="tpu_custom_call" | custom-call | tf_op jit(solution)/shard_map/reduce_return/pallas_call | solution.py:292
  174.8 0.0 copy-start.5
  174.8 0.0 copy-start.6
  174.8 0.0 copy-start.7
  174.8 2.2 %multiply_bitcast_fusion = f32[1,96,2048]{2,1,0:T(8,128)} fusion(f32[96,2048]{1,0:T(8,128)} %get-tuple-element.17), kind=kLoop, calls=%fused_computation.10 | loop fusion | flops 196608 | bytes 1572864 | tf_op jit(solution)/shard_map/broadcast_in_dim | solution.py:338
  177.1 0.0 copy-done.5
  177.1 0.0 copy-done.6
  177.1 1.2 multiply_bitcast_fusion.1
  178.3 0.0 copy-done.7
  178.3 0.8 copy.14
  (1 shorter events, 0.0 us)
Async XLA Ops:
  0.6 39.6 %copy-start = (bf16[1,768,2048]{2,1,0:T(8,128)(2,1)S(1)}, bf16[1,768,2048]{2,1,0:T(8,128)(2,1)}, u32[]{:S(2)}) copy-start(bf16[1,768,2048]{2,1,0:T(8,128)(2,1)} %param.13) | copy-start | bytes 9437188
  2.3 1.0 copy-start.2
  3.3 1.0 copy-start.3
  31.7 4.5 %copy-start.1 = (bf16[4,128,2048]{2,1,0:T(8,128)(2,1)}, bf16[4,128,2048]{2,1,0:T(8,128)(2,1)S(1)}, u32[]{:S(2)}) copy-start(bf16[4,128,2048]{2,1,0:T(8,128)(2,1)S(1)} %get-tuple-element.11) | copy-start | bytes 6291460
  31.8 4.4 %copy-start.4 = (bf16[1,2048,768]{2,1,0:T(8,128)(2,1)S(1)}, bf16[1,2048,768]{2,1,0:T(8,128)(2,1)}, u32[]{:S(2)}) copy-start(bf16[1,2048,768]{2,1,0:T(8,128)(2,1)} %param.11) | copy-start | bytes 9437188
  174.8 2.3 %copy-start.5 = (f32[256,768]{1,0:T(8,128)S(1)}, f32[256,768]{1,0:T(8,128)}, u32[]{:S(2)}) copy-start(f32[256,768]{1,0:T(8,128)} %get-tuple-element.15) | copy-start | bytes 2359300
  174.8 2.2 %copy-start.6 = (f32[256,768]{1,0:T(8,128)S(1)}, f32[256,768]{1,0:T(8,128)}, u32[]{:S(2)}) copy-start(f32[256,768]{1,0:T(8,128)} %get-tuple-element.16) | copy-start | bytes 2359300
  174.8 3.5 %copy-start.7 = (bf16[128,2048]{1,0:T(8,128)(2,1)S(1)}, bf16[128,2048]{1,0:T(8,128)(2,1)}, u32[]{:S(2)}) copy-start(bf16[128,2048]{1,0:T(8,128)(2,1)} %get-tuple-element.27) | copy-start | bytes 1572868

commit v3 on v2

--- a/solution.py
+++ b/solution.py
@@ -117,7 +117,8 @@
     span, replicas, x_ref, scaled_ref, hidden_ref, dg_ref, du_ref, wg_ref, wu_ref,
     gate_out, up_out, down_out, tok_out,
     grad_a, grad_b, grad_c, near_a, near_b, near_c, sum_a, sum_b, sum_c, line_a, line_b, line_c, route, back,
-    near_send, near_recv, line_send, line_recv, back_send, back_recv,
+    grad_z, sum_z, line_z, total_z, cross_out, cross_in,
+    near_send, near_recv, line_send, line_recv, back_send, back_recv, cross_send, cross_recv,
 ):
     expert = lax.axis_index("expert")
     me = lax.axis_index("dp")
@@ -127,9 +128,10 @@
     partner = line * 2 + (1 - side)
     grads = (grad_a, grad_b, grad_c)
     nears = (near_a, near_b, near_c)
-    sums = (sum_a, sum_b, sum_c)
-    lines = (line_a, line_b, line_c)
-    outs = (gate_out, up_out, down_out)
+    sums = (sum_a, sum_b, sum_c, sum_z)
+    lines = (line_a, line_b, line_c, line_z)
+    half = down_out.shape[1] // 2
+    outs = (gate_out, up_out, down_out.at[:, half:])
     tensors = (2, 0, 1)
     lower = lax.rem(line + outer - 1, outer) * 2 + side
     upper = lax.rem(line + 1, outer) * 2 + side
@@ -142,8 +144,7 @@
 
     def order_at(i):
         j = i + jnp.where(i >= place, 1, 0)
-        half = j // 2
-        d = jnp.where(lax.rem(j, 2) == 0, outer - 1 - half, half)
+        d = jnp.where(lax.rem(j, 2) == 0, outer - 1 - j // 2, j // 2)
         return jnp.where(i == outer - 1, line, d)
 
     def near_copy(t, d):
@@ -153,11 +154,11 @@
             device_id={"dp": partner}, device_id_type=MESH,
         )
 
-    def line_copy(t, d):
+    def line_copy(t, d, source=None):
         following = jnp.where(d > line, line + 1, line - 1)
         slot = jnp.where((d < line) & (d == following), outer, d)
         return pltpu.make_async_remote_copy(
-            src_ref=sums[t].at[d], dst_ref=lines[t].at[slot],
+            src_ref=sums[t].at[d] if source is None else source, dst_ref=lines[t].at[slot],
             send_sem=line_send.at[t, d], recv_sem=line_recv.at[t, slot],
             device_id={"dp": following * 2 + side}, device_id_type=MESH,
         )
@@ -180,32 +181,70 @@
     def outer_product(left, right):
         return lax.dot_general(left, right, (((0,), (0,)), ((), ())), preferred_element_type=F32)
 
+    def is_fed(d):
+        return ((d > line) & (line > 0)) | ((d < line) & (line < outer - 1))
+
+    cross = pltpu.make_async_remote_copy(
+        src_ref=cross_out, dst_ref=cross_in, send_sem=cross_send, recv_sem=cross_recv,
+        device_id={"dp": partner}, device_id_type=MESH,
+    )
     units = hidden_ref.shape[1]
     width = units // 2
     shard = units // replicas
-    for part in range(2):
-        product = outer_product(hidden_ref[:, part * width : (part + 1) * width], scaled_ref[...])
-        for piece in range(width // shard):
-            grad_c[part * (width // shard) + piece] = product[piece * shard : (piece + 1) * shard].astype(BF16)
-
-    def start_down(i, carry):
-        near_copy(2, order_at(i)).start()
-        return carry
-
-    lax.fori_loop(0, outer, start_down, 0)
+
+    def down_product(target, columns):
+        for part in range(2):
+            product = outer_product(hidden_ref[:, part * width : (part + 1) * width], scaled_ref[:, columns])
+            for piece in range(width // shard):
+                target[part * (width // shard) + piece] = product[piece * shard : (piece + 1) * shard].astype(BF16)
+
+    def both(d):
+        return grad_z.at[pl.ds(d * 2, 2)]
+
+    down_product(grad_z, slice(0, half))
+
+    def start_line(i, carry):
+        d = order_at(i)
+
+        @pl.when(jnp.logical_not(is_fed(d)))
+        def _():
+            line_copy(3, d, both(d)).start()
+
+        return carry
+
+    lax.fori_loop(0, outer - 1, start_line, 0)
+    down_product(grad_c, slice(half, 2 * half))
+    near_copy(2, order_at(0)).start()
     feature = x_ref.shape[1] // replicas
 
-    def start_pair(i, carry):
+    def make_pair(i, carry):
         d = order_at(i)
         columns = x_ref[:, pl.ds(pl.multiple_of(d * 2 * feature, 2 * feature), 2 * feature)]
         for t, right in ((0, dg_ref), (1, du_ref)):
             product = outer_product(columns, right[...])
             grads[t][d * 2] = product[:feature].astype(BF16)
             grads[t][d * 2 + 1] = product[feature:].astype(BF16)
-            near_copy(t, d).start()
-        return carry
-
-    lax.fori_loop(0, outer, start_pair, 0)
+
+            @pl.when(i == 0)
+            def _():
+                near_copy(t, d).start()
+
+        return carry
+
+    lax.fori_loop(0, outer, make_pair, 0)
+
+    def feed_line(i, carry):
+        d = order_at(i)
+
+        @pl.when(is_fed(d))
+        def _():
+            line_wait(3, d)
+            sum_z[d] = (grad_z[pl.ds(d * 2, 2)].astype(F32) + line_z[d].astype(F32)).astype(BF16)
+            line_copy(3, d).start()
+
+        return carry
+
+    lax.fori_loop(0, outer - 1, feed_line, 0)
     rows = tok_out.shape[0]
 
     def route_block(step):
@@ -226,9 +265,28 @@
 
     def forward(i, carry):
         d = order_at(i)
-        fed = ((d > line) & (line > 0)) | ((d < line) & (line < outer - 1))
+        fed = is_fed(d)
+
+        @pl.when(i == max(outer // 2 - 1, 0))
+        def _():
+            total_z[...] = grad_z[pl.ds(line * 2, 2)].astype(F32)
+
+            @pl.when(line > 0)
+            def _():
+                line_wait(3, line)
+                total_z[...] += line_z[line].astype(F32)
+
+            @pl.when(line < outer - 1)
+            def _():
+                line_wait(3, outer)
+                total_z[...] += line_z[outer].astype(F32)
+
+            cross_out[...] = total_z[1 - side].astype(BF16)
+            cross.start()
+
         for t in tensors:
             near_copy(t, d).wait_recv()
+            near_copy(t, order_at(i + 1)).start()
 
             @pl.when(fed)
             def _():
@@ -252,6 +310,8 @@
     for step in range(1, span):
         total = total + back[step].astype(F32)
     tok_out[...] = total.astype(BF16)
+    cross.wait_recv()
+    down_out[:, :half] = total_z[side] + cross_in[...].astype(F32)
     for t in tensors:
         near_copy(t, line).wait_recv()
         outs[t][...] = grads[t][me].astype(F32) + nears[t][line].astype(F32)
@@ -271,13 +331,15 @@
         for t in range(3):
             near_copy(t, d).wait_send()
 
-            @pl.when(i < outer - 1)
-            def _():
+        @pl.when(i < outer - 1)
+        def _():
+            for t in range(4):
                 line_copy(t, d).wait_send()
 
         return carry
 
     lax.fori_loop(0, outer, finish, 0)
+    cross.wait_send()
     for step in range(1, span):
         back_copy(step).wait_send()
 
@@ -289,17 +351,26 @@
     width, units = x.shape[1], hidden.shape[1]
     rows = x.shape[0] // span
     shards = [(width // replicas, units)] * 2 + [(units // replicas, width)]
+    parts = shards[:2] + [(units // replicas, width // 2)]
     return pl.pallas_call(
         functools.partial(reduce_kernel, span, replicas),
         out_shape=tuple(jax.ShapeDtypeStruct(s, F32) for s in shards)
         + (jax.ShapeDtypeStruct((rows, width), BF16),),
         in_specs=[whole] * 7,
         out_specs=[whole] * 4,
-        scratch_shapes=[pltpu.VMEM((replicas,) + s, BF16) for s in shards]
-        + [pltpu.VMEM((outer,) + s, BF16) for s in shards] * 2
-        + [pltpu.VMEM((outer + 1,) + s, BF16) for s in shards]
+        scratch_shapes=[pltpu.VMEM((replicas,) + s, BF16) for s in parts]
+        + [pltpu.VMEM((outer,) + s, BF16) for s in parts] * 2
+        + [pltpu.VMEM((outer + 1,) + s, BF16) for s in parts]
         + [pltpu.VMEM((span, rows, width), BF16)] * 2
-        + [dma((3, outer)), dma((3, outer)), dma((3, outer)), dma((3, outer + 1)), dma((span,)), dma((span,))],
+        + [
+            pltpu.VMEM((replicas,) + parts[2], BF16),
+            pltpu.VMEM((outer, 2) + parts[2], BF16),
+            pltpu.VMEM((outer + 1, 2) + parts[2], BF16),
+            pltpu.VMEM((2,) + parts[2], F32),
+            pltpu.VMEM(parts[2], BF16),
+            pltpu.VMEM(parts[2], BF16),
+        ]
+        + [dma((3, outer)), dma((3, outer)), dma((4, outer)), dma((4, outer + 1)), dma((span,)), dma((span,)), dma, dma],
         compiler_params=pltpu.CompilerParams(
             collective_id=1, has_side_effects=True, vmem_limit_bytes=60 << 20
         ),

time: 183 us -> 166 us (0.907); the launches traced: 179 us -> 166 us
  Pallas kernels: 158 us -> 145 us
    pallas_call x1, Pallas kernels: 131 us -> 118 us  [reduce_return(): pl.pallas_call(functools.partial(reduce_kernel, span, replicas), out_shap...]
where the time goes in v3:
time: 166 us
  Pallas kernels  145 us (87%)
  matrix products  10 us (6%)
  other arithmetic  7.3 us (4%)
  local copies, waits for them, and re-layouts  2.91 us (2%)
    pallas_call x1, Pallas kernels, reduce_return(): pl.pallas_call(functools.partial(reduce_kernel, span, replicas), out_shap...  118 us
    pallas_call x1, Pallas kernels, dispatch(): pl.pallas_call(functools.partial(dispatch_kernel, span, parts), out_shape...  27.4 us
    dot_general x1, matrix products, body(): pre_up = jnp.dot(x, w_up, preferred_element_type=F32)  4.4 us
    dot_general x1, matrix products, body(): lax.dot_general(scaled, w_down, (((1,), (1,)), ((), ())), preferred_eleme...  3.8 us

profile of v3, /device:TPU:20, one launch (start us, length us, event | category | flops | bytes accessed | tf_op | source)
XLA Modules:
  0.0 165.9 jit_solution(7053754428269527092)
XLA Ops:
  0.6 0.0 copy-start
  0.7 0.8 convert_multiply_fusion
  1.5 0.8 select_reduce_fusion.1.c_ref
  2.3 0.0 copy-start.2
  2.3 1.0 copy-done.2
  3.3 0.0 copy-start.3
  3.3 1.0 copy-done.3
  4.4 27.4 %dispatch.1 = (bf16[4,128,2048]{2,1,0:T(8,128)(2,1)S(1)}, bf16[4,128,2048]{2,1,0:T(8,128)(2,1)S(1)}, f32[4,8,128]{2,1,0:T(8,128)S(1)}) custom-call(bf16[128,2048]{1,0:T(8,128)(2,1)S(1)} %copy-done.2, bf16[128,2048]{1,0:T(8,128)(2,1)S(1)} %copy-done.3, f32[8,128]{1,0:T(8,128)S(1)} %select_reduce_fusion.1.c_ref), custom_call_target="tpu_custom_call" | custom-call | tf_op jit(solution)/shard_map/dispatch/pallas_call | solution.py:96
  31.7 0.0 copy-start.1
  31.7 0.1 select_reduce_fusion
  31.8 0.0 copy-start.4
  31.8 4.4 %fusion.4 = f32[512,768]{1,0:T(8,128)S(1)} fusion(bf16[512,2048]{1,0:T(8,128)(2,1)S(1)} %bitcast.27, bf16[1,2048,768]{2,1,0:T(8,128)(2,1)} %param.12), kind=kOutput, calls=%fused_computation.18 | convolution fusion | flops 1610612736 | bytes 6815744 | tf_op jit(solution)/shard_map/dot_general | solution.py:398
  36.2 0.0 copy-done.1
  36.2 0.0 copy-done.4
  36.3 1.8 %fusion.6 = f32[512,768]{1,0:T(8,128)S(1)} fusion(bf16[512,2048]{1,0:T(8,128)(2,1)S(1)} %bitcast.28, bf16[1,2048,768]{2,1,0:T(8,128)(2,1)S(1)} %copy-done.4), kind=kOutput, calls=%fused_computation.20 | convolution fusion | flops 1610612736 | bytes 6815744 | tf_op jit(solution)/shard_map/dot_general | solution.py:397
  38.1 1.7 %fusion.scaled_ref = bf16[512,2048]{1,0:T(8,128)(2,1)} fusion(f32[512]{0:T(512)S(1)} %bitcast.33, bf16[4,128,2048]{2,1,0:T(8,128)(2,1)S(1)} %get-tuple-element.13), kind=kLoop, calls=%fused_computation.1 | loop fusion | flops 3145728 | bytes 4196352 | tf_op jit(solution)/shard_map/convert_element_type | solution.py:396
  39.8 0.4 multiply_convert_fusion
  40.2 0.0 copy-done
  40.2 3.8 %multiply_convert_fusion.1 = (bf16[512,768]{1,0:T(8,128)(2,1)}, bf16[512,768]{1,0:T(8,128)(2,1)}, bf16[512,768]{1,0:T(8,128)(2,1)}) fusion(f32[512,768]{1,0:T(8,128)S(1)} %fusion.6, f32[512,768]{1,0:T(8,128)S(1)} %fusion.4, bf16[512,2048]{1,0:T(8,128)(2,1)S(1)} %bitcast.32, bf16[1,768,2048]{2,1,0:T(8,128)(2,1)S(1)} %copy-done), kind=kOutput, calls=%fused_computation.5 | convolution fusion | flops 1616510976 | bytes 10747904 | tf_op jit(solution)/shard_map/dot_general | solution.py:402
  44.0 117.6 %reduce_return.1 = (f32[256,768]{1,0:T(8,128)}, f32[256,768]{1,0:T(8,128)}, f32[96,2048]{1,0:T(8,128)}, bf16[128,2048]{1,0:T(8,128)(2,1)}) custom-call(bf16[512,2048]{1,0:T(8,128)(2,1)} %bitcast.29, bf16[512,2048]{1,0:T(8,128)(2,1)} %fusion.scaled_ref, bf16[512,768]{1,0:T(8,128)(2,1)} %get-tuple-element.20.hidden_ref, ...), custom_call_target="tpu_custom_call" | custom-call | tf_op jit(solution)/shard_map/reduce_return/pallas_call | solution.py:355
  161.6 0.0 copy-start.5
  161.7 0.0 copy-start.6
  161.7 0.0 copy-start.7
  161.7 2.2 %multiply_bitcast_fusion = f32[1,96,2048]{2,1,0:T(8,128)} fusion(f32[96,2048]{1,0:T(8,128)} %get-tuple-element.17), kind=kLoop, calls=%fused_computation.10 | loop fusion | flops 196608 | bytes 1572864 | tf_op jit(solution)/shard_map/broadcast_in_dim | solution.py:409
  163.9 0.0 copy-done.5
  163.9 0.0 copy-done.6
  163.9 1.2 multiply_bitcast_fusion.1
  165.1 0.0 copy-done.7
  165.1 0.8 copy.14
  (1 shorter events, 0.0 us)
Async XLA Ops:
  0.6 39.6 %copy-start = (bf16[1,768,2048]{2,1,0:T(8,128)(2,1)S(1)}, bf16[1,768,2048]{2,1,0:T(8,128)(2,1)}, u32[]{:S(2)}) copy-start(bf16[1,768,2048]{2,1,0:T(8,128)(2,1)} %param.13) | copy-start | bytes 9437188
  2.3 1.0 copy-start.2
  3.3 1.0 copy-start.3
  31.7 4.5 %copy-start.1 = (bf16[4,128,2048]{2,1,0:T(8,128)(2,1)}, bf16[4,128,2048]{2,1,0:T(8,128)(2,1)S(1)}, u32[]{:S(2)}) copy-start(bf16[4,128,2048]{2,1,0:T(8,128)(2,1)S(1)} %get-tuple-element.11) | copy-start | bytes 6291460
  31.8 4.4 %copy-start.4 = (bf16[1,2048,768]{2,1,0:T(8,128)(2,1)S(1)}, bf16[1,2048,768]{2,1,0:T(8,128)(2,1)}, u32[]{:S(2)}) copy-start(bf16[1,2048,768]{2,1,0:T(8,128)(2,1)} %param.11) | copy-start | bytes 9437188
  161.6 2.3 %copy-start.5 = (f32[256,768]{1,0:T(8,128)S(1)}, f32[256,768]{1,0:T(8,128)}, u32[]{:S(2)}) copy-start(f32[256,768]{1,0:T(8,128)} %get-tuple-element.15) | copy-start | bytes 2359300
  161.7 2.2 %copy-start.6 = (f32[256,768]{1,0:T(8,128)S(1)}, f32[256,768]{1,0:T(8,128)}, u32[]{:S(2)}) copy-start(f32[256,768]{1,0:T(8,128)} %get-tuple-element.16) | copy-start | bytes 2359300
  161.7 3.5 %copy-start.7 = (bf16[128,2048]{1,0:T(8,128)(2,1)S(1)}, bf16[128,2048]{1,0:T(8,128)(2,1)}, u32[]{:S(2)}) copy-start(bf16[128,2048]{1,0:T(8,128)(2,1)} %get-tuple-element.27) | copy-start | bytes 1572868

commit v4 on v3

--- a/solution.py
+++ b/solution.py
@@ -284,7 +284,7 @@
             cross_out[...] = total_z[1 - side].astype(BF16)
             cross.start()
 
-        for t in tensors:
+        for k, t in enumerate(tensors):
             near_copy(t, d).wait_recv()
             near_copy(t, order_at(i + 1)).start()
 
@@ -299,6 +299,14 @@
             def _():
                 sums[t][d] = (grads[t][d * 2 + side].astype(F32) + nears[t][d].astype(F32)).astype(BF16)
 
+            if k == 0:
+
+                @pl.when(i > 0)
+                def _():
+                    line_copy(tensors[2], order_at(i - 1)).wait_send()
+
+            else:
+                line_copy(tensors[k - 1], d).wait_send()
             line_copy(t, d).start()
         return carry
 
@@ -333,12 +341,13 @@
 
         @pl.when(i < outer - 1)
         def _():
-            for t in range(4):
-                line_copy(t, d).wait_send()
+            line_copy(3, d).wait_send()
 
         return carry
 
     lax.fori_loop(0, outer, finish, 0)
+    if outer > 1:
+        line_copy(tensors[2], order_at(outer - 2)).wait_send()
     cross.wait_send()
     for step in range(1, span):
         back_copy(step).wait_send()

time: 166 us -> 175 us (1.054)
  Pallas kernels: 145 us -> 154 us
    pallas_call x1, Pallas kernels: 118 us -> 126 us  [reduce_return(): pl.pallas_call(functools.partial(reduce_kernel, span, replicas), out_shap...]
where the time goes in v4:
time: 175 us
  Pallas kernels  154 us (88%)
  matrix products  10 us (6%)
  other arithmetic  7.3 us (4%)
  local copies, waits for them, and re-layouts  2.91 us (2%)
    pallas_call x1, Pallas kernels, reduce_return(): pl.pallas_call(functools.partial(reduce_kernel, span, replicas), out_shap...  126 us
    pallas_call x1, Pallas kernels, dispatch(): pl.pallas_call(functools.partial(dispatch_kernel, span, parts), out_shape...  27.4 us
    dot_general x1, matrix products, body(): pre_up = jnp.dot(x, w_up, preferred_element_type=F32)  4.4 us
    dot_general x1, matrix products, body(): lax.dot_general(scaled, w_down, (((1,), (1,)), ((), ())), preferred_eleme...  3.8 us

profile of v4, /device:TPU:20, one launch (start us, length us, event | category | flops | bytes accessed | tf_op | source)
XLA Modules:
  0.0 174.8 jit_solution(13371454522180699634)
XLA Ops:
  0.6 0.0 copy-start
  0.7 0.8 convert_multiply_fusion
  1.5 0.8 select_reduce_fusion.1.c_ref
  2.3 0.0 copy-start.2
  2.3 1.0 copy-done.2
  3.3 0.0 copy-start.3
  3.3 1.0 copy-done.3
  4.4 27.4 %dispatch.1 = (bf16[4,128,2048]{2,1,0:T(8,128)(2,1)S(1)}, bf16[4,128,2048]{2,1,0:T(8,128)(2,1)S(1)}, f32[4,8,128]{2,1,0:T(8,128)S(1)}) custom-call(bf16[128,2048]{1,0:T(8,128)(2,1)S(1)} %copy-done.2, bf16[128,2048]{1,0:T(8,128)(2,1)S(1)} %copy-done.3, f32[8,128]{1,0:T(8,128)S(1)} %select_reduce_fusion.1.c_ref), custom_call_target="tpu_custom_call" | custom-call | tf_op jit(solution)/shard_map/dispatch/pallas_call | solution.py:96
  31.7 0.0 copy-start.1
  31.7 0.1 select_reduce_fusion
  31.8 0.0 copy-start.4
  31.8 4.4 %fusion.4 = f32[512,768]{1,0:T(8,128)S(1)} fusion(bf16[512,2048]{1,0:T(8,128)(2,1)S(1)} %bitcast.27, bf16[1,2048,768]{2,1,0:T(8,128)(2,1)} %param.12), kind=kOutput, calls=%fused_computation.18 | convolution fusion | flops 1610612736 | bytes 6815744 | tf_op jit(solution)/shard_map/dot_general | solution.py:407
  36.2 0.0 copy-done.1
  36.2 0.0 copy-done.4
  36.3 1.8 %fusion.6 = f32[512,768]{1,0:T(8,128)S(1)} fusion(bf16[512,2048]{1,0:T(8,128)(2,1)S(1)} %bitcast.28, bf16[1,2048,768]{2,1,0:T(8,128)(2,1)S(1)} %copy-done.4), kind=kOutput, calls=%fused_computation.20 | convolution fusion | flops 1610612736 | bytes 6815744 | tf_op jit(solution)/shard_map/dot_general | solution.py:406
  38.1 1.7 fusion.scaled_ref
  39.8 0.4 multiply_convert_fusion
  40.2 0.0 copy-done
  40.2 3.8 %multiply_convert_fusion.1 = (bf16[512,768]{1,0:T(8,128)(2,1)}, bf16[512,768]{1,0:T(8,128)(2,1)}, bf16[512,768]{1,0:T(8,128)(2,1)}) fusion(f32[512,768]{1,0:T(8,128)S(1)} %fusion.6, f32[512,768]{1,0:T(8,128)S(1)} %fusion.4, bf16[512,2048]{1,0:T(8,128)(2,1)S(1)} %bitcast.32, bf16[1,768,2048]{2,1,0:T(8,128)(2,1)S(1)} %copy-done), kind=kOutput, calls=%fused_computation.5 | convolution fusion | flops 1616510976 | bytes 10747904 | tf_op jit(solution)/shard_map/dot_general | solution.py:411
  44.0 126.5 %reduce_return.1 = (f32[256,768]{1,0:T(8,128)}, f32[256,768]{1,0:T(8,128)}, f32[96,2048]{1,0:T(8,128)}, bf16[128,2048]{1,0:T(8,128)(2,1)}) custom-call(bf16[512,2048]{1,0:T(8,128)(2,1)} %bitcast.29, bf16[512,2048]{1,0:T(8,128)(2,1)} %fusion.scaled_ref, bf16[512,768]{1,0:T(8,128)(2,1)} %get-tuple-element.20.hidden_ref, ...), custom_call_target="tpu_custom_call" | custom-call | tf_op jit(solution)/shard_map/reduce_return/pallas_call | solution.py:364
  170.5 0.0 copy-start.5
  170.5 0.0 copy-start.6
  170.5 0.0 copy-start.7
  170.5 2.2 %multiply_bitcast_fusion = f32[1,96,2048]{2,1,0:T(8,128)} fusion(f32[96,2048]{1,0:T(8,128)} %get-tuple-element.17), kind=kLoop, calls=%fused_computation.10 | loop fusion | flops 196608 | bytes 1572864 | tf_op jit(solution)/shard_map/broadcast_in_dim | solution.py:418
  172.7 0.0 copy-done.5
  172.7 0.0 copy-done.6
  172.7 1.2 multiply_bitcast_fusion.1
  174.0 0.0 copy-done.7
  174.0 0.8 copy.14
  (1 shorter events, 0.0 us)
Async XLA Ops:
  0.6 39.6 %copy-start = (bf16[1,768,2048]{2,1,0:T(8,128)(2,1)S(1)}, bf16[1,768,2048]{2,1,0:T(8,128)(2,1)}, u32[]{:S(2)}) copy-start(bf16[1,768,2048]{2,1,0:T(8,128)(2,1)} %param.13) | copy-start | bytes 9437188
  2.3 1.0 copy-start.2
  3.3 1.0 copy-start.3
  31.7 4.5 %copy-start.1 = (bf16[4,128,2048]{2,1,0:T(8,128)(2,1)}, bf16[4,128,2048]{2,1,0:T(8,128)(2,1)S(1)}, u32[]{:S(2)}) copy-start(bf16[4,128,2048]{2,1,0:T(8,128)(2,1)S(1)} %get-tuple-element.11) | copy-start | bytes 6291460
  31.8 4.4 %copy-start.4 = (bf16[1,2048,768]{2,1,0:T(8,128)(2,1)S(1)}, bf16[1,2048,768]{2,1,0:T(8,128)(2,1)}, u32[]{:S(2)}) copy-start(bf16[1,2048,768]{2,1,0:T(8,128)(2,1)} %param.11) | copy-start | bytes 9437188
  170.5 2.3 %copy-start.5 = (f32[256,768]{1,0:T(8,128)S(1)}, f32[256,768]{1,0:T(8,128)}, u32[]{:S(2)}) copy-start(f32[256,768]{1,0:T(8,128)} %get-tuple-element.15) | copy-start | bytes 2359300
  170.5 2.2 %copy-start.6 = (f32[256,768]{1,0:T(8,128)S(1)}, f32[256,768]{1,0:T(8,128)}, u32[]{:S(2)}) copy-start(f32[256,768]{1,0:T(8,128)} %get-tuple-element.16) | copy-start | bytes 2359300
  170.5 3.5 %copy-start.7 = (bf16[128,2048]{1,0:T(8,128)(2,1)S(1)}, bf16[128,2048]{1,0:T(8,128)(2,1)}, u32[]{:S(2)}) copy-start(bf16[128,2048]{1,0:T(8,128)(2,1)} %get-tuple-element.27) | copy-start | bytes 1572868

commit v5 on v3

--- a/solution.py
+++ b/solution.py
@@ -20,7 +20,7 @@
 
 
 def dispatch_kernel(
-    span, parts, x_ref, g_ref, c_ref, xs_ref, gs_ref, cs_ref,
+    span, parts, x_ref, g_ref, c_ref, wg_ref, wu_ref, xs_ref, gs_ref, cs_ref, gate_ref, up_ref,
     own_sem, core_send, core_recv, chip_send, chip_recv, fwd_send, fwd_recv, c_send, c_recv,
 ):
     me = lax.axis_index("expert")
@@ -68,26 +68,56 @@
     mine = pltpu.make_async_copy(c_ref, cs_ref.at[me], own_sem.at[2])
     mine.start()
     locals_.append(mine)
-    for array, part, step, copy in chip_copies:
-        copy.wait_recv()
-        owner = lax.rem(chip + chips - step, chips) * 2 + core
-        block = piece(pairs[array][1].at[owner], part)
-        forward = pltpu.make_async_remote_copy(
-            src_ref=block, dst_ref=block,
-            send_sem=fwd_send.at[array, part, step], recv_sem=fwd_recv.at[array, part, step],
-            device_id={"expert": other}, device_id_type=MESH,
-        )
-        forward.start()
-        forwards.append(forward)
+
+    def project(owner, block):
+        gate_ref[owner] = jnp.dot(block[...], wg_ref[...], preferred_element_type=F32)
+        up_ref[owner] = jnp.dot(block[...], wu_ref[...], preferred_element_type=F32)
+
+    project(me, x_ref)
+    started[span - 1].wait_recv()
+    project(other, xs_ref.at[other])
+    passed = {}
+    for array in range(2):
+        for number, part, step, copy in chip_copies:
+            if number == array:
+                copy.wait_recv()
+                owner = lax.rem(chip + chips - step, chips) * 2 + core
+                block = piece(pairs[array][1].at[owner], part)
+                forward = pltpu.make_async_remote_copy(
+                    src_ref=block, dst_ref=block,
+                    send_sem=fwd_send.at[array, part, step], recv_sem=fwd_recv.at[array, part, step],
+                    device_id={"expert": other}, device_id_type=MESH,
+                )
+                forward.start()
+                passed[array, part, step] = forward
+        if array == 0:
+            for step in range(1, chips):
+                there = lax.rem(chip + chips - step, chips) * 2
+                project(there + core, xs_ref.at[there + core])
+                for part in range(parts):
+                    owner = there + (1 - core)
+                    block = piece(xs_ref.at[owner], part)
+                    pltpu.make_async_remote_copy(
+                        src_ref=block, dst_ref=block,
+                        send_sem=fwd_send.at[0, part, step], recv_sem=fwd_recv.at[0, part, step],
+                        device_id={"expert": other}, device_id_type=MESH,
+                    ).wait_recv()
+                project(there + (1 - core), xs_ref.at[there + (1 - core)])
     for copy in locals_:
         copy.wait()
     for _, _, _, copy in chip_copies:
         copy.wait_send()
-    for copy in started + forwards:
-        copy.wait()
-
-
-def dispatch(tokens, d_out, coef, span):
+    for at, copy in enumerate(started):
+        copy.wait_send()
+        if at != span - 1:
+            copy.wait_recv()
+    for (array, _, _), forward in passed.items():
+        forward.wait_send()
+        if array == 1:
+            forward.wait_recv()
+
+
+def dispatch(tokens, d_out, coef, w_gate, w_up, span):
     parts = 4
     rows, width = tokens.shape
     dma = pltpu.SemaphoreType.DMA
@@ -99,9 +129,11 @@
             jax.ShapeDtypeStruct((span, rows, width), BF16),
             jax.ShapeDtypeStruct((span, rows, width), BF16),
             jax.ShapeDtypeStruct((span,) + coef.shape, F32),
+            jax.ShapeDtypeStruct((span, rows, w_gate.shape[1]), F32),
+            jax.ShapeDtypeStruct((span, rows, w_gate.shape[1]), F32),
         ),
-        in_specs=[whole] * 3,
-        out_specs=[whole] * 3,
+        in_specs=[whole] * 5,
+        out_specs=[whole] * 5,
         scratch_shapes=[
             dma((3,)), dma((2,)), dma((2,)), dma((2, parts, chips)), dma((2, parts, chips)),
             dma((2, parts, chips)), dma((2, parts, chips)), dma((span,)), dma((span,)),
@@ -110,7 +142,7 @@
             collective_id=0, has_side_effects=True, vmem_limit_bytes=40 << 20
         ),
         name="dispatch",
-    )(tokens, d_out, coef)
+    )(tokens, d_out, coef, w_gate, w_up)
 
 
 def reduce_kernel(
@@ -130,8 +162,8 @@
     nears = (near_a, near_b, near_c)
     sums = (sum_a, sum_b, sum_c, sum_z)
     lines = (line_a, line_b, line_c, line_z)
-    half = down_out.shape[1] // 2
-    outs = (gate_out, up_out, down_out.at[:, half:])
+    cut = down_out.shape[1] // 4
+    outs = (gate_out, up_out, down_out.at[:, cut:])
     tensors = (2, 0, 1)
     lower = lax.rem(line + outer - 1, outer) * 2 + side
     upper = lax.rem(line + 1, outer) * 2 + side
@@ -201,7 +233,7 @@
     def both(d):
         return grad_z.at[pl.ds(d * 2, 2)]
 
-    down_product(grad_z, slice(0, half))
+    down_product(grad_z, slice(0, cut))
 
     def start_line(i, carry):
         d = order_at(i)
@@ -213,7 +245,7 @@
         return carry
 
     lax.fori_loop(0, outer - 1, start_line, 0)
-    down_product(grad_c, slice(half, 2 * half))
+    down_product(grad_c, slice(cut, down_out.shape[1]))
     near_copy(2, order_at(0)).start()
     feature = x_ref.shape[1] // replicas
 
@@ -311,7 +343,7 @@
         total = total + back[step].astype(F32)
     tok_out[...] = total.astype(BF16)
     cross.wait_recv()
-    down_out[:, :half] = total_z[side] + cross_in[...].astype(F32)
+    down_out[:, :cut] = total_z[side] + cross_in[...].astype(F32)
     for t in tensors:
         near_copy(t, line).wait_recv()
         outs[t][...] = grads[t][me].astype(F32) + nears[t][line].astype(F32)
@@ -351,7 +383,8 @@
     width, units = x.shape[1], hidden.shape[1]
     rows = x.shape[0] // span
     shards = [(width // replicas, units)] * 2 + [(units // replicas, width)]
-    parts = shards[:2] + [(units // replicas, width // 2)]
+    parts = shards[:2] + [(units // replicas, width - width // 4)]
+    early = (units // replicas, width // 4)
     return pl.pallas_call(
         functools.partial(reduce_kernel, span, replicas),
         out_shape=tuple(jax.ShapeDtypeStruct(s, F32) for s in shards)
@@ -363,12 +396,12 @@
         + [pltpu.VMEM((outer + 1,) + s, BF16) for s in parts]
         + [pltpu.VMEM((span, rows, width), BF16)] * 2
         + [
-            pltpu.VMEM((replicas,) + parts[2], BF16),
-            pltpu.VMEM((outer, 2) + parts[2], BF16),
-            pltpu.VMEM((outer + 1, 2) + parts[2], BF16),
-            pltpu.VMEM((2,) + parts[2], F32),
-            pltpu.VMEM(parts[2], BF16),
-            pltpu.VMEM(parts[2], BF16),
+            pltpu.VMEM((replicas,) + early, BF16),
+            pltpu.VMEM((outer, 2) + early, BF16),
+            pltpu.VMEM((outer + 1, 2) + early, BF16),
+            pltpu.VMEM((2,) + early, F32),
+            pltpu.VMEM(early, BF16),
+            pltpu.VMEM(early, BF16),
         ]
         + [dma((3, outer)), dma((3, outer)), dma((4, outer)), dma((4, outer + 1)), dma((span,)), dma((span,)), dma, dma],
         compiler_params=pltpu.CompilerParams(
@@ -390,12 +423,12 @@
     coef = jnp.sum(
         jnp.where(places[:, None, None] == routes[None], gate_value[None], 0.0), axis=2
     )
-    xs, gs, cs = dispatch(tokens, d_out, coef, span)
+    xs, gs, cs, pre_gate, pre_up = dispatch(tokens, d_out, coef, w_gate, w_up, span)
     x = xs.reshape(span * rows, width)
     weight = jnp.sum(jnp.where(places[None, :, None] == me, cs, 0.0), axis=1).reshape(span * rows, 1)
     scaled = (weight * gs.reshape(span * rows, width).astype(F32)).astype(BF16)
-    pre_gate = jnp.dot(x, w_gate, preferred_element_type=F32)
-    pre_up = jnp.dot(x, w_up, preferred_element_type=F32)
+    pre_gate = pre_gate.reshape(span * rows, hidden_units)
+    pre_up = pre_up.reshape(span * rows, hidden_units)
     sigmoid_gate = jax.nn.sigmoid(pre_gate)
     silu_gate = pre_gate * sigmoid_gate
     hidden = (silu_gate * pre_up).astype(BF16)

time: 166 us -> 158 us (0.952); the launches traced: 166 us -> 155 us
  Pallas kernels: 145 us -> 138 us
  matrix products: 10 us -> 3.74 us
  local copies, waits for them, and re-layouts: 2.91 us -> 4.79 us
    pallas_call x1, Pallas kernels: 118 us -> 109 us  [reduce_return(): pl.pallas_call(functools.partial(reduce_kernel, span, replicas), out_shap...]
    dot_general x2 -> x0, matrix products: 6.21 us -> none  [the longest x1 4.4 us: body(): pre_up = jnp.dot(x, w_up, preferred_element_type=F32)]
    pallas_call x1, Pallas kernels: 27.4 us -> 29.3 us  [dispatch(): pl.pallas_call(functools.partial(dispatch_kernel, span, parts), out_shape...]
    unnamed x17, local copies, waits for them, and re-layouts: 2.91 us -> 4.79 us
where the time goes in v5:
time: 158 us; the launch traced here: 155 us
  Pallas kernels  138 us (87%)
  other arithmetic  7.43 us (5%)
  local copies, waits for them, and re-layouts  4.79 us (3%)
  matrix products  3.74 us (2%)
    pallas_call x1, Pallas kernels, reduce_return(): pl.pallas_call(functools.partial(reduce_kernel, span, replicas), out_shap...  109 us
    pallas_call x1, Pallas kernels, dispatch(): pl.pallas_call(functools.partial(dispatch_kernel, span, parts), out_shape...  29.3 us
    unnamed x17, local copies, waits for them, and re-layouts  4.79 us
    dot_general x1, matrix products, body(): lax.dot_general(scaled, w_down, (((1,), (1,)), ((), ())), preferred_eleme...  3.74 us

profile of v5, /device:TPU:20, one launch (start us, length us, event | category | flops | bytes accessed | tf_op | source)
XLA Modules:
  0.0 154.7 jit_solution(9774047698485790975)
XLA Ops:
  0.6 0.0 copy-start
  0.7 0.8 convert_multiply_fusion
  1.5 0.8 select_reduce_fusion.1.c_ref
  2.3 0.0 copy-start.1
  2.3 1.9 %copy-done.1 = bf16[1,2048,768]{2,1,0:T(8,128)(2,1)S(1)} copy-done((bf16[1,2048,768]{2,1,0:T(8,128)(2,1)S(1)}, bf16[1,2048,768]{2,1,0:T(8,128)(2,1)}, u32[]{:S(2)}) %copy-start.1) | copy-done | bytes 3145752
  4.2 0.0 copy-start.3
  4.2 1.0 copy-done.3
  5.2 0.0 copy-start.4
  5.2 1.0 copy-done.4
  6.3 29.3 %dispatch.1 = (bf16[4,128,2048]{2,1,0:T(8,128)(2,1)S(1)}, bf16[4,128,2048]{2,1,0:T(8,128)(2,1)S(1)}, f32[4,8,128]{2,1,0:T(8,128)S(1)}, f32[4,128,768]{2,1,0:T(8,128)S(1)}, f32[4,128,768]{2,1,0:T(8,128)S(1)}) custom-call(bf16[128,2048]{1,0:T(8,128)(2,1)S(1)} %copy-done.3, bf16[128,2048]{1,0:T(8,128)(2,1)S(1)} %copy-done.4, ...), custom_call_target="tpu_custom_call" | custom-call | tf_op jit(solution)/shard_map/dispatch/pallas_call | solution.py:126
  35.5 0.0 copy-start.2
  35.5 0.1 select_reduce_fusion
  35.6 1.8 %fusion.scaled_ref = bf16[512,2048]{1,0:T(8,128)(2,1)} fusion(f32[512]{0:T(512)S(1)} %bitcast.60, bf16[4,128,2048]{2,1,0:T(8,128)(2,1)S(1)} %get-tuple-element.15), kind=kLoop, calls=%fused_computation.1 | loop fusion | flops 3145728 | bytes 4196352 | tf_op jit(solution)/shard_map/convert_element_type | solution.py:429
  37.5 0.0 copy-done.2
  37.5 0.4 multiply_convert_fusion
  37.9 0.0 copy-done
  37.9 3.7 %multiply_convert_fusion.1 = (bf16[512,768]{1,0:T(8,128)(2,1)}, bf16[512,768]{1,0:T(8,128)(2,1)}, bf16[512,768]{1,0:T(8,128)(2,1)}) fusion(f32[4,128,768]{2,1,0:T(8,128)S(1)} %get-tuple-element.16, f32[4,128,768]{2,1,0:T(8,128)S(1)} %get-tuple-element.17, bf16[512,2048]{1,0:T(8,128)(2,1)S(1)} %bitcast.59, bf16[1,768,2048]{2,1,0:T(8,128)(2,1)S(1)} %copy-done), kind=kOutput, calls=%fused_computation.18 | convolution fusion | flops 1616510976 | bytes 10747904 | tf_op jit(solution)/shard_map/dot_general | solution.py:435
  41.6 108.7 %reduce_return.1 = (f32[256,768]{1,0:T(8,128)}, f32[256,768]{1,0:T(8,128)}, f32[96,2048]{1,0:T(8,128)}, bf16[128,2048]{1,0:T(8,128)(2,1)}) custom-call(bf16[512,2048]{1,0:T(8,128)(2,1)} %bitcast.56, bf16[512,2048]{1,0:T(8,128)(2,1)} %fusion.scaled_ref, bf16[512,768]{1,0:T(8,128)(2,1)} %get-tuple-element.24.hidden_ref, ...), custom_call_target="tpu_custom_call" | custom-call | tf_op jit(solution)/shard_map/reduce_return/pallas_call | solution.py:388
  150.4 0.0 copy-start.5
  150.4 0.0 copy-start.6
  150.4 0.0 copy-start.7
  150.4 2.2 %multiply_bitcast_fusion = f32[1,96,2048]{2,1,0:T(8,128)} fusion(f32[96,2048]{1,0:T(8,128)} %get-tuple-element.21), kind=kLoop, calls=%fused_computation.19 | loop fusion | flops 196608 | bytes 1572864 | tf_op jit(solution)/shard_map/broadcast_in_dim | solution.py:442
  152.6 0.0 copy-done.5
  152.6 0.0 copy-done.6
  152.6 1.2 multiply_bitcast_fusion.1
  153.9 0.0 copy-done.7
  153.9 0.8 copy.14
  (1 shorter events, 0.0 us)
Async XLA Ops:
  0.6 37.2 %copy-start = (bf16[1,768,2048]{2,1,0:T(8,128)(2,1)S(1)}, bf16[1,768,2048]{2,1,0:T(8,128)(2,1)}, u32[]{:S(2)}) copy-start(bf16[1,768,2048]{2,1,0:T(8,128)(2,1)} %param.13) | copy-start | bytes 9437188
  2.3 1.9 %copy-start.1 = (bf16[1,2048,768]{2,1,0:T(8,128)(2,1)S(1)}, bf16[1,2048,768]{2,1,0:T(8,128)(2,1)}, u32[]{:S(2)}) copy-start(bf16[1,2048,768]{2,1,0:T(8,128)(2,1)} %param.11) | copy-start | bytes 9437188
  4.2 1.0 copy-start.3
  5.2 1.0 copy-start.4
  35.5 1.9 %copy-start.2 = (bf16[4,128,2048]{2,1,0:T(8,128)(2,1)}, bf16[4,128,2048]{2,1,0:T(8,128)(2,1)S(1)}, u32[]{:S(2)}) copy-start(bf16[4,128,2048]{2,1,0:T(8,128)(2,1)S(1)} %get-tuple-element.13) | copy-start | bytes 6291460
  150.4 2.3 %copy-start.5 = (f32[256,768]{1,0:T(8,128)S(1)}, f32[256,768]{1,0:T(8,128)}, u32[]{:S(2)}) copy-start(f32[256,768]{1,0:T(8,128)} %get-tuple-element.19) | copy-start | bytes 2359300
  150.4 2.2 %copy-start.6 = (f32[256,768]{1,0:T(8,128)S(1)}, f32[256,768]{1,0:T(8,128)}, u32[]{:S(2)}) copy-start(f32[256,768]{1,0:T(8,128)} %get-tuple-element.20) | copy-start | bytes 2359300
  150.4 3.5 %copy-start.7 = (bf16[128,2048]{1,0:T(8,128)(2,1)S(1)}, bf16[128,2048]{1,0:T(8,128)(2,1)}, u32[]{:S(2)}) copy-start(bf16[128,2048]{1,0:T(8,128)(2,1)} %get-tuple-element.31) | copy-start | bytes 1572868
